TPU v7x, 32 devices: a whole 2x2x4 slice. The times are simulated.
32 devices in a mesh: groups: 2 (over y), ctx: 8 (over z, x), mp: 2 (over core).
Axes of the slice: x: 2, y: 2, z: 4, core: 2. Of those that a mesh axis runs over, the one named last changes fastest.
Arguments:
- inputs: bfloat16 [2048, 2048], P(('groups', 'ctx'), 'mp'), parts along dimension 0, may hold values from -6 to 6
- cotangent: bfloat16 [2048, 2048], P(('groups', 'ctx'), 'mp'), parts along dimension 0, may hold values from -0.1875 to 0.1875
- filters: float32 [1024, 24], P('ctx'), may hold values from -0.1875 to 0.1875
- mixing: float32 [24, 2048], P(None, 'mp'), may hold values from -1.25 to 1.25
- ar_coef: float32 [3, 2048], P(None, 'mp'), may hold values from -3 to 3
Outputs:
- outputs: bfloat16 [2048, 2048], P(('groups', 'ctx'), 'mp'), parts along dimension 0
- grad_mixing: float32 [48, 2048], P('groups', 'mp'), parts along dimension 0
- grad_ar: float32 [6, 2048], P('groups', 'mp'), parts along dimension 0
There are 2 independent parts, one for each index of `groups`. A program takes and returns all parts, laid end to end along the dimension named above; an argument that names none is the same for every part. Nothing has to cross between parts.
All inputs are finite; a program needn't handle non-finite values.
Results may differ from a plain program's by a relative error of at most 0.001.
Values may be sent and summed in bfloat16 or wider, within the bound.
No kernel may reach another device: no remote copies, remote signals or barrier semaphores. Data moves between devices by JAX's collectives and lax.ppermute only.
A program may use at most 64 MiB of HBM per device.

v0:
```python
import math

import jax
import jax.numpy as jnp
from jax import lax
from jax.sharding import PartitionSpec as P

ORDER = 3


highest = lax.Precision.HIGHEST


def phase_tables(seq_len):
    radix_len = math.gcd(seq_len, 128)
    outer_len = 2 * seq_len // radix_len
    half_outer = outer_len // 2
    total_len = 2 * seq_len
    low_index = jnp.arange(half_outer, dtype=jnp.int32)
    outer_index = jnp.arange(outer_len, dtype=jnp.int32)
    radix_index = jnp.arange(radix_len, dtype=jnp.int32)
    outer_angle = (low_index[:, None] * outer_index[None, :] % outer_len).astype(jnp.float32) * (
        2.0 * math.pi / outer_len
    )
    twist_angle = (outer_index[:, None] * radix_index[None, :] % total_len).astype(jnp.float32) * (
        2.0 * math.pi / total_len
    )
    radix_angle = (radix_index[:, None] * radix_index[None, :] % radix_len).astype(jnp.float32) * (
        2.0 * math.pi / radix_len
    )
    return (
        jnp.cos(outer_angle),
        jnp.sin(outer_angle),
        jnp.cos(twist_angle),
        jnp.sin(twist_angle),
        jnp.cos(radix_angle),
        jnp.sin(radix_angle),
    )


def forward_spectrum(signal, tables):
    outer_cos, outer_sin, twist_cos, twist_sin, radix_cos, radix_sin = tables
    channels = signal.shape[0]
    folded = signal.reshape(channels, outer_cos.shape[0], radix_cos.shape[0])
    first_real = jnp.einsum("chr,hk->ckr", folded, outer_cos, precision=highest)
    first_imag = -jnp.einsum("chr,hk->ckr", folded, outer_sin, precision=highest)
    turned_real = first_real * twist_cos + first_imag * twist_sin
    turned_imag = first_imag * twist_cos - first_real * twist_sin
    spec_real = jnp.einsum("ckr,rq->ckq", turned_real, radix_cos, precision=highest) + jnp.einsum(
        "ckr,rq->ckq", turned_imag, radix_sin, precision=highest
    )
    spec_imag = jnp.einsum("ckr,rq->ckq", turned_imag, radix_cos, precision=highest) - jnp.einsum(
        "ckr,rq->ckq", turned_real, radix_sin, precision=highest
    )
    return (spec_real, spec_imag)


def inverse_spectrum(spec_real, spec_imag, tables):
    outer_cos, outer_sin, twist_cos, twist_sin, radix_cos, radix_sin = tables
    back_real = jnp.einsum("ckq,rq->ckr", spec_real, radix_cos, precision=highest) - jnp.einsum(
        "ckq,rq->ckr", spec_imag, radix_sin, precision=highest
    )
    back_imag = jnp.einsum("ckq,rq->ckr", spec_real, radix_sin, precision=highest) + jnp.einsum(
        "ckq,rq->ckr", spec_imag, radix_cos, precision=highest
    )
    untwist_real = back_real * twist_cos - back_imag * twist_sin
    untwist_imag = back_real * twist_sin + back_imag * twist_cos
    folded = jnp.einsum("ckr,hk->chr", untwist_real, outer_cos, precision=highest) - jnp.einsum(
        "ckr,hk->chr", untwist_imag, outer_sin, precision=highest
    )
    channels = folded.shape[0]
    total_len = 2 * folded.shape[1] * folded.shape[2]
    return folded.reshape(channels, -1) / total_len


def local(inputs, cotangent, filters, mixing, ar_coef):
    tok_rows, local_width = inputs.shape
    ctx_count = lax.axis_size("ctx")
    ctx_place = lax.axis_index("ctx")
    narrow = local_width // ctx_count
    seq_len = tok_rows * ctx_count
    tables = phase_tables(seq_len)
    seq_cols = lax.all_to_all(inputs.T, "ctx", split_axis=0, concat_axis=1, tiled=True)
    signal = seq_cols.astype(jnp.float32)
    filter_all = lax.all_gather(filters, "ctx", axis=0, tiled=True)
    mix_local = lax.dynamic_slice_in_dim(mixing, ctx_place * narrow, narrow, 1)
    kernel = jnp.einsum("lk,kc->cl", filter_all, mix_local, precision=highest)
    sig_real, sig_imag = forward_spectrum(signal, tables)
    ker_real, ker_imag = forward_spectrum(kernel, tables)
    convolved = inverse_spectrum(
        ker_real * sig_real - ker_imag * sig_imag, ker_real * sig_imag + ker_imag * sig_real, tables
    )
    cot_cols = lax.all_to_all(cotangent.T, "ctx", split_axis=0, concat_axis=1, tiled=True)
    cot_real, cot_imag = forward_spectrum(cot_cols.astype(jnp.float32), tables)
    lagged = inverse_spectrum(
        cot_real * sig_real + cot_imag * sig_imag, cot_imag * sig_real - cot_real * sig_imag, tables
    )
    ar_local = lax.dynamic_slice_in_dim(ar_coef, ctx_place * narrow, narrow, 1)
    padded = jnp.pad(signal, ((0, 0), (ORDER, 0)))
    autoreg = jnp.zeros_like(signal)
    for lag_step in range(1, ORDER + 1):
        autoreg = (
            autoreg
            + ar_local[lag_step - 1][:, None]
            * padded[:, ORDER - lag_step : ORDER - lag_step + seq_len]
        )
    out_cols = (convolved + autoreg).astype(jnp.bfloat16)
    outputs = lax.all_to_all(out_cols, "ctx", split_axis=1, concat_axis=0, tiled=True).T
    mix_piece = jnp.einsum("lk,cl->kc", filter_all, lagged, precision=highest)
    grad_mixing, grad_ar = (
        lax.all_gather(mix_piece, "ctx", axis=1, tiled=True),
        lax.all_gather(lagged[:, 1 : ORDER + 1].T, "ctx", axis=1, tiled=True),
    )
    return (outputs, grad_mixing, grad_ar)


def solution(mesh):
    return jax.shard_map(
        local,
        mesh=mesh,
        in_specs=(
            P(("groups", "ctx"), "mp"),
            P(("groups", "ctx"), "mp"),
            P("ctx", None),
            P(None, "mp"),
            P(None, "mp"),
        ),
        out_specs=(P(("groups", "ctx"), "mp"), P("groups", "mp"), P("groups", "mp")),
        check_vma=False,
    )
```

profile of v0, /device:TPU:0, one launch (start us, length us, event | category | flops | bytes accessed | tf_op | source)
XLA Modules:
  0.0 162.8 jit_solution(16318002603742689494)
XLA Ops:
  0.6 0.0 copy-start
  0.6 1.8 %copy.72 = bf16[128,1024]{0,1:T(8,128)(2,1)} copy(bf16[128,1024]{1,0:T(8,128)(2,1)} %param.5) | data formatting | bytes 524288 | tf_op args[0]
  2.5 7.3 %all-to-all-start = ((bf16[8,128,128]{2,1,0:T(8,128)(2,1)}), bf16[8,128,128]{2,1,0:T(8,128)(2,1)S(1)}, u32[]{:S(2)}, u32[]{:S(2)}) async-start(bf16[8,128,128]{2,1,0:T(8,128)(2,1)} %bitcast.7), calls=%async_computation | async-start | bytes 524288 | tf_op jit(solution)/shard_map/all_to_all | solution.py:83
  9.8 0.0 copy-start.3
  9.8 0.1 fusion.110
  9.8 0.6 copy-done.3
  10.5 32.3 %all_gather.9 = f32[1024,24]{0,1:T(8,128)S(1)} all-gather(f32[128,24]{0,1:T(8,128)S(1)} %copy-done.3), channel_id=1, replica_groups=mesh['groups'=2,'ctx'=8,'mp'=2] {'ctx'}, dimensions={0}, use_global_device_ids=true | all-gather | bytes 110592 | tf_op jit(solution)/shard_map/all_gather | solution.py:85
  42.8 0.0 copy-done
  42.8 0.6 convolution_bitcast_fusion
  43.4 0.0 copy-start.2
  43.4 0.1 copy.95
  43.5 0.8 copy-done.2
  44.3 0.8 copy.84
  45.2 0.7 constant_dynamic-slice_fusion
  45.9 2.1 %convolution_negate_fusion = f32[16,128,128]{2,0,1:T(8,128)} fusion(f32[128,8,128]{2,1,0:T(8,128)S(1)} %bitcast.144), kind=kOutput, calls=%fused_computation | convolution fusion | flops 25429760 | bytes 1572864 | tf_op jit(solution)/shard_map/chr,hk->ckr/dot_general | solution.py:46
  47.9 0.0 all-to-all-done
  47.9 4.4 %all-to-all-start.2 = ((bf16[8,128,128]{2,1,0:T(8,128)(2,1)}), bf16[8,128,128]{2,1,0:T(8,128)(2,1)S(1)}, u32[]{:S(2)}, u32[]{:S(2)}) async-start(bf16[8,128,128]{2,1,0:T(8,128)(2,1)} %bitcast.20), calls=%async_computation.2 | async-start | bytes 524288 | tf_op jit(solution)/shard_map/all_to_all | solution.py:93
  52.3 0.7 convolution_negate_fusion.2
  53.0 0.7 fusion.33
  53.7 6.7 %all-to-all-done.2 = bf16[8,128,128]{2,1,0:T(8,128)(2,1)S(1)} async-done(((bf16[8,128,128]{2,1,0:T(8,128)(2,1)}), bf16[8,128,128]{2,1,0:T(8,128)(2,1)S(1)}, u32[]{:S(2)}, u32[]{:S(2)}) %all-to-all-start.2) | async-done | bytes 262176 | tf_op jit(solution)/shard_map/all_to_all | solution.py:93
  60.4 0.7 convolution_negate_fusion.1
  61.1 0.7 fusion.30
  61.8 0.0 copy-done.1
  61.8 1.9 %add_bitcast_fusion = (f32[128,16,128]{2,1,0:T(8,128)S(1)}, f32[128,16,128]{2,1,0:T(8,128)S(1)}, f32[128,16,128]{2,1,0:T(8,128)S(1)}, f32[128,16,128]{2,1,0:T(8,...) fusion(f32[16,128,128]{2,0,1:T(8,128)S(1)} %convolution_negate_fusion.1, ...), kind=kOutput, calls=%fused_computation.30 | convolution fusion | flops 29886208 | bytes 12075008 | tf_op jit(solution)/shard_map/chr,hk->ckr/dot_general | solution.py:45
  63.7 1.4 fusion.24
  65.1 1.4 fusion.20
  66.6 1.4 convolution_add_fusion.4
  68.0 1.4 convolution_subtract_fusion.4
  69.5 1.4 fusion.18
  70.9 1.6 %fusion.14 = f32[128,16,128]{2,0,1:T(8,128)S(1)} fusion(f32[128,16,128]{2,1,0:T(8,128)S(1)} %get-tuple-element.24), kind=kOutput, calls=%fused_computation.45 | convolution fusion | flops 402882560 | bytes 2097152 | tf_op jit(solution)/shard_map/ckr,rq->ckq/dot_general | solution.py:52
  72.5 1.4 convolution_add_fusion.3
  74.0 1.4 fusion.8
  75.4 1.4 fusion.12
  76.8 1.4 convolution_subtract_fusion.1
  78.3 1.4 convolution_subtract_fusion.3
  79.7 1.8 %multiply_subtract_fusion.1 = (f32[128,16,128]{2,0,1:T(8,128)S(1)}, f32[128,16,128]{2,0,1:T(8,128)S(1)}, f32[128,16,128]{2,0,1:T(8,128)S(1)}, f32[128,16,128]{2,0,1:T(8,128)S(1)}) fusion(f32[128,16,128]{2,0,1:T(8,128)S(1)} %convolution_subtract_fusion.3, f32[128,16,128]{2,0,1:T(8,128)S(1)} %convolution_subtract_fusion.1, ...), kind=kOutput, calls=%fused_computation.27 | convolution fusion | flops 406290432 | bytes 11534336 | tf_op jit(solution)/shard_map/ckr,rq->ckq/dot_general | solution.py:49
  81.6 1.2 fusion.58
  82.8 1.7 %fusion.45 = f32[128,16,128]{2,0,1:T(8,128)S(1)} fusion(f32[128,16,128]{2,0,1:T(8,128)S(1)} %get-tuple-element.20), kind=kOutput, calls=%fused_computation.86 | convolution fusion | flops 402882560 | bytes 2097152 | tf_op jit(solution)/shard_map/ckq,rq->ckr/dot_general | solution.py:63
  84.4 1.2 fusion.53
  85.7 1.2 fusion.40
  86.9 1.3 convolution_subtract_fusion.2
  88.2 1.2 convolution_add_fusion.2
  89.4 1.2 convolution_subtract_fusion
  90.7 1.7 %multiply_add_fusion = (f32[128,16,128]{2,0,1:T(8,128)S(1)}, f32[128,16,128]{2,0,1:T(8,128)S(1)}, f32[128,16,128]{2,0,1:T(8,128)S(1)}, f32[128,16,128]{2,0,1:T(8,128)S(1)}) fusion(f32[128,16,128]{2,0,1:T(8,128)S(1)} %convolution_subtract_fusion, f32[16,128]{1,0:T(8,128)S(1)} %get-tuple-element.31, f32[16,128]{1,0:T(8,128)S(1)} %get-tuple-element.32, ...), kind=kOutput, calls=%fused_computation.25 | convolution fusion | flops 406290432 | bytes 9453568 | tf_op jit(solution)/shard_map/ckq,rq->ckr/dot_general | solution.py:63
  92.4 1.2 fusion.3
  93.6 1.2 fusion.6
  94.8 0.2 copy.73
  95.0 0.1 pad_convert_fusion
  95.1 1.4 fusion.1
  96.5 0.4 fusion.26
  96.9 0.8 copy.82
  97.8 3.4 %all-to-all-start.1 = ((bf16[128,8,128]{0,2,1:T(8,128)(2,1)}), bf16[128,8,128]{0,2,1:T(8,128)(2,1)S(1)}, u32[]{:S(2)}, u32[]{:S(2)}) async-start(bf16[128,8,128]{0,2,1:T(8,128)(2,1)} %bitcast.15), calls=%async_computation.1 | async-start | bytes 524288 | tf_op jit(solution)/shard_map/all_to_all | solution.py:108
  101.2 1.2 fusion
  102.4 0.1 copy.153
  102.5 0.1 slice.31
  102.6 0.1 copy.94
  102.6 26.6 %all_gather.11 = f32[3,1024]{1,0:T(4,128)S(1)} all-gather(f32[3,128]{1,0:T(4,128)S(1)} %bitcast.153), channel_id=1, replica_groups=mesh['groups'=2,'ctx'=8,'mp'=2] {'ctx'}, dimensions={1}, use_global_device_ids=true | all-gather | bytes 13824 | tf_op jit(solution)/shard_map/all_gather | solution.py:112
  129.3 0.5 convolution_bitcast_fusion.1
  129.8 30.6 %all_gather.10 = f32[24,1024]{1,0:T(8,128)S(1)} all-gather(f32[24,128]{1,0:T(8,128)S(1)} %convolution_bitcast_fusion.1), channel_id=1, replica_groups=mesh['groups'=2,'ctx'=8,'mp'=2] {'ctx'}, dimensions={1}, use_global_device_ids=true | all-gather | bytes 110592 | tf_op jit(solution)/shard_map/all_gather | solution.py:111
  160.3 0.0 all-to-all-done.1
  160.3 0.2 copy.83
  160.5 0.9 copy.93
  161.4 0.6 copy.157
  162.0 0.6 copy.158
  (3 shorter events, 0.1 us)
Async XLA Ops:
  0.6 42.1 %copy-start = (f32[24,1024]{1,0:T(8,128)S(1)}, f32[24,1024]{1,0:T(8,128)}, u32[]{:S(2)}) copy-start(f32[24,1024]{1,0:T(8,128)} %param.8) | copy-start | bytes 294916
  2.5 45.4 %all-to-all-start = ((bf16[8,128,128]{2,1,0:T(8,128)(2,1)}), bf16[8,128,128]{2,1,0:T(8,128)(2,1)S(1)}, u32[]{:S(2)}, u32[]{:S(2)}) async-start(bf16[8,128,128]{2,1,0:T(8,128)(2,1)} %bitcast.7), calls=%async_computation | async-start | bytes 524288 | tf_op jit(solution)/shard_map/all_to_all | solution.py:83
  9.8 0.7 copy-start.3
  43.4 1.0 copy-start.2
  47.9 12.5 %all-to-all-start.2 = ((bf16[8,128,128]{2,1,0:T(8,128)(2,1)}), bf16[8,128,128]{2,1,0:T(8,128)(2,1)S(1)}, u32[]{:S(2)}, u32[]{:S(2)}) async-start(bf16[8,128,128]{2,1,0:T(8,128)(2,1)} %bitcast.20), calls=%async_computation.2 | async-start | bytes 524288 | tf_op jit(solution)/shard_map/all_to_all | solution.py:93
  60.4 1.4 copy-start.1
  97.8 62.6 %all-to-all-start.1 = ((bf16[128,8,128]{0,2,1:T(8,128)(2,1)}), bf16[128,8,128]{0,2,1:T(8,128)(2,1)S(1)}, u32[]{:S(2)}, u32[]{:S(2)}) async-start(bf16[128,8,128]{0,2,1:T(8,128)(2,1)} %bitcast.15), calls=%async_computation.1 | async-start | bytes 524288 | tf_op jit(solution)/shard_map/all_to_all | solution.py:108
where the time goes:
time: 166 us; the launch traced here: 163 us
  blocking collectives  89.5 us (54%)
  matrix products  41.2 us (25%)
  starting transfers between devices  15.1 us (9%)
  local copies, waits for them, and re-layouts  8.53 us (5%)
  waiting for transfers between devices  6.7 us (4%)
    all_gather x1, blocking collectives, local(): filter_all = lax.all_gather(filters, 'ctx', axis=0, tiled=True)  32.3 us
    all_gather x1, blocking collectives, local(): lax.all_gather(mix_piece, 'ctx', axis=1, tiled=True)  30.6 us
    all_gather x1, blocking collectives, local(): lax.all_gather(lagged[:, 1:ORDER + 1].T, 'ctx', axis=1, tiled=True)  26.6 us
    all_to_all x1, starting transfers between devices, local(): lax.all_to_all(inputs.T, 'ctx', split_axis=0, concat_axis=1, tiled=True)  7.28 us
    all_to_all x1, waiting for transfers between devices, local(): lax.all_to_all(cotangent.T, 'ctx', split_axis=0, concat_axis=1, tiled=True)  6.7 us
    unnamed x17, local copies, waits for them, and re-layouts  6.57 us
    dot_general x3, matrix products, forward_spectrum(): jnp.einsum('ckr,rq->ckq', turned_imag, radix_sin, precision=highest)  4.67 us
    dot_general x3, matrix products, forward_spectrum(): jnp.einsum('ckr,rq->ckq', turned_imag, radix_cos, precision=highest)  4.48 us
  transfers between devices with their start and end apart: 3, of which 1 were waited for; matrix products, arithmetic and copies ran while one was open for 5% of the time, Pallas kernels for 0%

commit v1 on v0

--- a/solution.py
+++ b/solution.py
@@ -1,13 +1,20 @@
+import functools
 import math
 
 import jax
 import jax.numpy as jnp
+import numpy as np
 from jax import lax
+from jax.experimental import pallas as pl
+from jax.experimental.pallas import tpu as pltpu
 from jax.sharding import PartitionSpec as P
 
 ORDER = 3
-
-
+LANES = 128
+ROWS = 16
+
+f32 = jnp.float32
+bf16 = jnp.bfloat16
 highest = lax.Precision.HIGHEST
 
 
@@ -73,7 +80,7 @@
     return folded.reshape(channels, -1) / total_len
 
 
-def local(inputs, cotangent, filters, mixing, ar_coef):
+def local_general(inputs, cotangent, filters, mixing, ar_coef):
     tok_rows, local_width = inputs.shape
     ctx_count = lax.axis_size("ctx")
     ctx_place = lax.axis_index("ctx")
@@ -114,6 +121,329 @@
     return (outputs, grad_mixing, grad_ar)
 
 
+def split_pair(value):
+    high = value.astype(bf16)
+    return high, (value - high.astype(f32)).astype(bf16)
+
+
+def turn(count, k):
+    angle = math.pi * (k + 0.5) / count
+    return math.cos(angle), math.sin(angle)
+
+
+def half_forward(xs):
+    n = len(xs)
+    if n == 1:
+        return [(xs[0], None)]
+    even, odd = half_forward(xs[0::2]), half_forward(xs[1::2])
+    low, high = [], []
+    for k in range(n // 2):
+        c, s = turn(n, k)
+        er, ei = even[k]
+        orr, oi = odd[k]
+        if oi is None:
+            tr, ti = orr * c, orr * (-s)
+            low.append((er + tr, ti))
+            high.append((er - tr, ti))
+        else:
+            tr, ti = orr * c + oi * s, oi * c - orr * s
+            low.append((er + tr, ei + ti))
+            high.append((er - tr, ti - ei))
+    return low + high[::-1]
+
+
+def half_inverse(us):
+    n = len(us)
+    if n == 1:
+        return [us[0][0]]
+    even, odd = [], []
+    for k in range(n // 2):
+        c, s = turn(n, k)
+        (ar, ai), (br, bi) = us[k], us[n - 1 - k]
+        dr, di = ar - br, ai + bi
+        if n == 2:
+            even.append((ar + br, None))
+            odd.append((dr * c - di * s, None))
+        else:
+            even.append((ar + br, ai - bi))
+            odd.append((dr * c - di * s, dr * s + di * c))
+    out = [None] * n
+    out[0::2] = half_inverse(even)
+    out[1::2] = half_inverse(odd)
+    return out
+
+
+def dft_constants(half, radix):
+    index = np.arange(radix)
+    angle = 2.0 * np.pi * (index[:, None] * index[None, :] % radix) / radix
+    c, s = np.cos(angle), np.sin(angle)
+    forward = np.block([[c, s], [-s, c]])
+
+    def stacked(matrix):
+        matrix = matrix.astype(np.float32)
+        high = matrix.astype(jnp.bfloat16)
+        low = (matrix - high.astype(np.float32)).astype(jnp.bfloat16)
+        return np.concatenate([high, low], axis=0)
+
+    theta = 2.0 * np.pi * index[:, None] * (np.arange(half)[None, :] + 0.5) / (2 * half * radix)
+    twist = np.concatenate([np.cos(theta), np.sin(theta)], axis=1).astype(np.float32)
+    return stacked(forward), stacked(forward.T), twist, np.ascontiguousarray(twist.T)
+
+
+def dot(a, b):
+    return jnp.dot(a, b, preferred_element_type=f32)
+
+
+def outer_forward(src_ref, tw_ref, high_ref, low_ref, half, radix):
+    for r in range(0, radix, ROWS):
+        parts = half_forward([src_ref[h, r : r + ROWS, :].astype(f32) for h in range(half)])
+        for k, (re, im) in enumerate(parts):
+            c, s = tw_ref[r : r + ROWS, k : k + 1], tw_ref[r : r + ROWS, half + k : half + k + 1]
+            lanes = slice(k * LANES, (k + 1) * LANES)
+            for base, value in ((0, re * c + im * s), (radix, im * c - re * s)):
+                high, low = split_pair(value)
+                high_ref[base + r : base + r + ROWS, lanes] = high
+                low_ref[base + r : base + r + ROWS, lanes] = low
+
+
+def inner_dft(w_ref, high_ref, low_ref, lanes):
+    both = w_ref.shape[0] // 2
+    first = dot(w_ref[...], high_ref[:, lanes])
+    return first[:both] + first[both:] + dot(w_ref[:both, :], low_ref[:, lanes])
+
+
+def pack_kernel(x_ref, g_ref, f_ref, first_ref, second_ref, *, count):
+    tok = x_ref.shape[0]
+    high, low = split_pair(f_ref[...].T)
+    taps = high.shape[0]
+    pieces = jnp.concatenate([high.astype(f32), low.astype(f32)], axis=0).astype(bf16)
+    for j in range(count):
+        lanes = slice(j * LANES, (j + 1) * LANES)
+        first_ref[j, 0:tok, :] = x_ref[:, lanes]
+        first_ref[j, tok : tok + 2 * taps, :] = pieces
+        second_ref[j] = g_ref[:, lanes]
+
+
+def conv_kernel(
+    place_ref,
+    recv_ref,
+    mix_ref,
+    ar_ref,
+    wf_ref,
+    wi_ref,
+    tw_ref,
+    twt_ref,
+    y_ref,
+    spec_ref,
+    taps_ref,
+    a_high,
+    a_low,
+    b_high,
+    b_low,
+    *,
+    half,
+    radix,
+    kp,
+):
+    taps = mix_ref.shape[0]
+    order = ar_ref.shape[0]
+    width = 2 * radix
+    blocks = []
+    for h in range(half):
+        both = recv_ref[h, radix : radix + 2 * taps, :].astype(f32)
+        value = both[:taps] + both[taps:]
+        extra = jnp.zeros((kp - taps, radix), f32)
+        if h == 0:
+            row = lax.broadcasted_iota(jnp.int32, extra.shape, 0)
+            lane = lax.broadcasted_iota(jnp.int32, extra.shape, 1)
+            extra = jnp.where((row < order) & (lane == row + 1), 1.0, extra)
+        blocks.append(jnp.concatenate([value, extra], axis=0))
+    for k, (re, im) in enumerate(half_forward(blocks)):
+        c, s = twt_ref[k : k + 1, :], twt_ref[half + k : half + k + 1, :]
+        value = jnp.concatenate([re * c + im * s, im * c - re * s], axis=1)
+        high, low = split_pair(value)
+        a_high[k * kp : (k + 1) * kp, 0:width] = high
+        a_low[k * kp : (k + 1) * kp, 0:width] = low
+    n_rows = half * kp
+    filt = (
+        dot(a_high[0:n_rows, 0:width], wi_ref[0:width, :])
+        + dot(a_low[0:n_rows, 0:width], wi_ref[0:width, :])
+        + dot(a_high[0:n_rows, 0:width], wi_ref[width : 2 * width, :])
+    )
+    f_high, f_low = split_pair(filt)
+    for k in range(half):
+        rows = slice(k * kp, (k + 1) * kp)
+        lanes = slice(k * width, (k + 1) * width)
+        taps_ref[0:kp, lanes] = f_high[rows]
+        taps_ref[kp : 2 * kp, lanes] = f_low[rows]
+    weights = jnp.concatenate(
+        [mix_ref[...], ar_ref[...], jnp.zeros((kp - taps - order, LANES), f32)], axis=0
+    ) * (1.0 / (half * radix))
+    m_high, m_low = split_pair(weights)
+    zero = jnp.zeros_like(m_high)
+
+    def diagonal(m):
+        return jnp.concatenate(
+            [jnp.concatenate([m, zero], axis=1), jnp.concatenate([zero, m], axis=1)], axis=0
+        )
+
+    d_high, d_low = diagonal(m_high), diagonal(m_low)
+    mixer = jnp.concatenate([d_high, d_high, d_low], axis=0)
+
+    outer_forward(recv_ref, tw_ref, b_high, b_low, half, radix)
+    for m in range(half // 2):
+        lanes = slice(m * 2 * LANES, (m + 1) * 2 * LANES)
+        rows = slice(2 * m * kp, 2 * (m + 1) * kp)
+        spec = inner_dft(wf_ref, b_high, b_low, lanes)
+        spec_ref[:, lanes] = spec
+        ker = lax.dot_general(
+            jnp.concatenate([f_high[rows], f_low[rows], f_high[rows]], axis=0),
+            mixer,
+            (((0,), (0,)), ((), ())),
+            preferred_element_type=f32,
+        )
+        sr, si, kr, ki = spec[:radix], spec[radix:], ker[:radix], ker[radix:]
+        for base, value in ((0, sr * kr - si * ki), (radix, sr * ki + si * kr)):
+            high, low = split_pair(value)
+            a_high[base : base + radix, lanes] = high
+            a_low[base : base + radix, lanes] = low
+    backs = []
+    for m in range(half // 2):
+        lanes = slice(m * 2 * LANES, (m + 1) * 2 * LANES)
+        backs.append(inner_dft(wi_ref, a_high, a_low, lanes))
+    for r in range(0, radix, ROWS):
+        us = []
+        for k in range(half):
+            lanes = slice((k % 2) * LANES, (k % 2 + 1) * LANES)
+            gr = backs[k // 2][r : r + ROWS, lanes]
+            gi = backs[k // 2][radix + r : radix + r + ROWS, lanes]
+            c, s = tw_ref[r : r + ROWS, k : k + 1], tw_ref[r : r + ROWS, half + k : half + k + 1]
+            us.append((gr * c - gi * s, gr * s + gi * c))
+        for h, value in enumerate(half_inverse(us)):
+            y_ref[h, r : r + ROWS, :] = value.astype(bf16)
+
+
+def grad_kernel(recv_ref, spec_ref, taps_ref, wf_ref, tw_ref, out_ref, b_high, b_low, p_high, p_low, *, half, radix, kp):
+    outer_forward(recv_ref, tw_ref, b_high, b_low, half, radix)
+    for m in range(half // 2):
+        lanes = slice(m * 2 * LANES, (m + 1) * 2 * LANES)
+        cot = inner_dft(wf_ref, b_high, b_low, lanes)
+        spec = spec_ref[:, lanes]
+        cr, ci, sr, si = cot[:radix], cot[radix:], spec[:radix], spec[radix:]
+        for base, value in ((0, cr * sr + ci * si), (radix, ci * sr - cr * si)):
+            high, low = split_pair(value)
+            for side in range(2):
+                row = (2 * m + side) * 2 * radix + base
+                part = slice(side * LANES, (side + 1) * LANES)
+                p_high[row : row + radix, :] = high[:, part]
+                p_low[row : row + radix, :] = low[:, part]
+    first = dot(taps_ref[...], p_high[...])
+    grads = (first[:kp] + first[kp:] + dot(taps_ref[0:kp, :], p_low[...])) * (1.0 / (half * radix))
+    for j in range(out_ref.shape[0]):
+        out_ref[j] = grads
+
+
+def unpack_kernel(y_ref, g_ref, out_ref, mix_ref, ar_ref, *, count):
+    taps, order = mix_ref.shape[0], ar_ref.shape[0]
+    for j in range(count):
+        lanes = slice(j * LANES, (j + 1) * LANES)
+        out_ref[:, lanes] = y_ref[j]
+        mix_ref[:, lanes] = g_ref[j, 0:taps, :]
+        ar_ref[:, lanes] = g_ref[j, taps : taps + order, :]
+
+
+def shape_of(*dims, dtype=f32):
+    return jax.ShapeDtypeStruct(dims, dtype)
+
+
+def local_tiled(inputs, cotangent, filters, mixing, ar_coef):
+    tok_rows, local_width = inputs.shape
+    count = lax.axis_size("ctx")
+    taps, order = filters.shape[1], ar_coef.shape[0]
+    half, radix = count, tok_rows
+    kp = -(-(taps + order) // 8) * 8
+    wf, wi, twist, twist_t = dft_constants(half, radix)
+    rows = tok_rows + 2 * taps
+
+    first, second = pl.pallas_call(
+        functools.partial(pack_kernel, count=count),
+        out_shape=(
+            shape_of(count, rows, LANES, dtype=bf16),
+            shape_of(count, tok_rows, LANES, dtype=bf16),
+        ),
+        name="pack",
+    )(inputs, cotangent, filters)
+    swap = functools.partial(lax.all_to_all, axis_name="ctx", split_axis=0, concat_axis=0, tiled=True)
+    first = swap(first)
+    second = swap(second)
+
+    whole = lambda *dims: pl.BlockSpec(dims, lambda i, place: (0,) * len(dims))
+    place = lax.axis_index("ctx").astype(jnp.int32).reshape(1)
+    span = half * LANES
+    y_cols, spec, spectra = pl.pallas_call(
+        functools.partial(conv_kernel, half=half, radix=radix, kp=kp),
+        out_shape=(
+            shape_of(count, tok_rows, LANES, dtype=bf16),
+            shape_of(2 * radix, span),
+            shape_of(2 * kp, half * 2 * radix, dtype=bf16),
+        ),
+        grid_spec=pltpu.PrefetchScalarGridSpec(
+            num_scalar_prefetch=1,
+            grid=(1,),
+            in_specs=[
+                whole(count, rows, LANES),
+                pl.BlockSpec((taps, LANES), lambda i, place: (0, place[0])),
+                pl.BlockSpec((order, LANES), lambda i, place: (0, place[0])),
+                whole(*wf.shape),
+                whole(*wi.shape),
+                whole(*twist.shape),
+                whole(*twist_t.shape),
+            ],
+            out_specs=(
+                whole(count, tok_rows, LANES),
+                whole(2 * radix, span),
+                whole(2 * kp, half * 2 * radix),
+            ),
+            scratch_shapes=[pltpu.VMEM((2 * radix, span), bf16)] * 4,
+        ),
+        cost_estimate=pl.CostEstimate(flops=3_000_000_000, bytes_accessed=3_000_000, transcendentals=0),
+        name="conv",
+    )(place, first, mixing, ar_coef, wf, wi, twist, twist_t)
+    y_rows = swap(y_cols)
+
+    grads = pl.pallas_call(
+        functools.partial(grad_kernel, half=half, radix=radix, kp=kp),
+        out_shape=shape_of(count, kp, LANES),
+        scratch_shapes=[pltpu.VMEM((2 * radix, span), bf16)] * 2
+        + [pltpu.VMEM((half * 2 * radix, LANES), bf16)] * 2,
+        cost_estimate=pl.CostEstimate(flops=1_500_000_000, bytes_accessed=3_000_000, transcendentals=0),
+        name="grads",
+    )(second, spec, spectra, wf, twist)
+    grads = swap(grads)
+
+    return pl.pallas_call(
+        functools.partial(unpack_kernel, count=count),
+        out_shape=(
+            shape_of(tok_rows, local_width, dtype=bf16),
+            shape_of(taps, local_width),
+            shape_of(order, local_width),
+        ),
+        name="unpack",
+    )(y_rows, grads)
+
+
+def local(inputs, cotangent, filters, mixing, ar_coef):
+    tok_rows, local_width = inputs.shape
+    count = lax.axis_size("ctx")
+    tiled = (
+        local_width == count * LANES
+        and tok_rows == LANES
+        and count in (2, 4, 8, 16)
+        and filters.shape[1] % 8 == 0
+    )
+    return (local_tiled if tiled else local_general)(inputs, cotangent, filters, mixing, ar_coef)
+
+
 def solution(mesh):
     return jax.shard_map(
         local,

time: 166 us -> 64 us (0.39); the launches traced: 163 us -> 63.4 us
  blocking collectives: 89.5 us -> 41.6 us
  matrix products: 41.2 us -> 0 us
  starting transfers between devices: 15.1 us -> 3.41 us
  Pallas kernels: 0 us -> 11 us
  local copies, waits for them, and re-layouts: 8.53 us -> 2.14 us
  waiting for transfers between devices: 6.7 us -> 4.66 us
    all_gather x3 -> x0, blocking collectives: 89.5 us -> none  [the longest x1 32.3 us: local(): filter_all = lax.all_gather(filters, 'ctx', axis=0, tiled=True)]
    all_to_all x0 -> x3, blocking collectives: none -> 41.6 us  [the longest x1 18.9 us: local_tiled(): first = swap(first)]
    dot_general x32 -> x0, matrix products: 41.2 us -> none  [the longest x3 4.67 us: forward_spectrum(): jnp.einsum('ckr,rq->ckq', turned_imag, radix_sin, precision=highest)]
    all_to_all x3 -> x1, starting transfers between devices: 15.1 us -> 3.41 us  [local_tiled(): second = swap(second)]
    pallas_call x0 -> x4, Pallas kernels: none -> 11 us  [the longest x1 3.83 us: local_tiled(): pl.pallas_call(functools.partial(conv_kernel, half=half, radix=radix, kp=...]
    unnamed x17 -> x5, local copies, waits for them, and re-layouts: 6.57 us -> 2.14 us
    all_to_all x3 -> x1, waiting for transfers between devices: 6.7 us -> 4.66 us  [local_tiled(): second = swap(second)]
  transfers between devices with their start and end apart: 3 -> 1, of which waited for: 1 -> 1; matrix products, arithmetic and copies ran while one was open for 5% -> 0% of each run, Pallas kernels for 0% -> 6%
where the time goes in v1:
time: 64 us; the launch traced here: 63.4 us
  blocking collectives  41.6 us (65%)
  Pallas kernels  11 us (17%)
  waiting for transfers between devices  4.66 us (7%)
  starting transfers between devices  3.41 us (5%)
  local copies, waits for them, and re-layouts  2.14 us (3%)
  between operations  0.65 us (1%)
    all_to_all x1, blocking collectives, local_tiled(): first = swap(first)  18.9 us
    all_to_all x1, blocking collectives, local_tiled(): grads = swap(grads)  11.5 us
    all_to_all x1, blocking collectives, local_tiled(): y_rows = swap(y_cols)  11.3 us
    all_to_all x1, waiting for transfers between devices, local_tiled(): second = swap(second)  4.66 us
    pallas_call x1, Pallas kernels, local_tiled(): pl.pallas_call(functools.partial(conv_kernel, half=half, radix=radix, kp=...  3.83 us
    all_to_all x1, starting transfers between devices, local_tiled(): second = swap(second)  3.41 us
    pallas_call x1, Pallas kernels, local_tiled(): pl.pallas_call(functools.partial(grad_kernel, half=half, radix=radix, kp=...  3.38 us
    unnamed x5, local copies, waits for them, and re-layouts  2.14 us
  transfers between devices with their start and end apart: 1, of which 1 were waited for; matrix products, arithmetic and copies ran while one was open for 0% of the time, Pallas kernels for 6%

profile of v1, /device:TPU:0, one launch (start us, length us, event | category | flops | bytes accessed | tf_op | source)
XLA Modules:
  0.0 63.4 jit_solution(3785433086356424231)
XLA Ops:
  0.6 1.4 %copy.12.f_ref = f32[128,24]{1,0:T(8,128)} copy(f32[128,24]{0,1:T(8,128)} %param.11) | data formatting | bytes 24576 | tf_op args[2]
  2.1 2.0 %pack.1 = (bf16[8,176,128]{2,1,0:T(8,128)(2,1)}, bf16[8,128,128]{2,1,0:T(8,128)(2,1)}) custom-call(bf16[128,1024]{1,0:T(8,128)(2,1)} %x_ref.1, bf16[128,1024]{1,0:T(8,128)(2,1)} %g_ref.1, f32[128,24]{1,0:T(8,128)} %copy.12.f_ref), custom_call_target="tpu_custom_call" | custom-call | tf_op jit(solution)/shard_map/pack/pallas_call | solution.py:368
  4.0 18.9 %all_to_all.20.recv_ref = bf16[8,176,128]{2,1,0:T(8,128)(2,1)} all-to-all(bf16[8,176,128]{2,1,0:T(8,128)(2,1)} %get-tuple-element.8), channel_id=1, replica_groups=mesh['groups'=2,'ctx'=8,'mp'=2] {'ctx'}, dimensions={0} | all-to-all | bytes 720896 | tf_op jit(solution)/shard_map/all_to_all | solution.py:377
  22.9 3.4 %all-to-all-start.2 = ((bf16[8,128,128]{2,1,0:T(8,128)(2,1)}), bf16[8,128,128]{2,1,0:T(8,128)(2,1)S(1)}, u32[]{:S(2)}, u32[]{:S(2)}) async-start(bf16[8,128,128]{2,1,0:T(8,128)(2,1)} %get-tuple-element.10), calls=%async_computation.2 | async-start | bytes 524288 | tf_op jit(solution)/shard_map/all_to_all | solution.py:378
  26.3 3.8 %conv.1 = (bf16[8,128,128]{2,1,0:T(8,128)(2,1)}, f32[256,1024]{1,0:T(8,128)}, bf16[64,2048]{1,0:T(8,128)(2,1)}) custom-call(s32[1]{0:T(128)} %bitcast.place_ref, bf16[8,176,128]{2,1,0:T(8,128)(2,1)} %all_to_all.20.recv_ref, f32[24,1024]{1,0:T(8,128)} %mix_ref.1, f32[3,1024]{1,0:T(4,128)} %ar_ref.1, bf16[512,256]{1,0:T(8,128)(2,1)} %constant.14.clone.wf_ref, ...), custom_call_target="tpu_custom_call" | custom-call | flops 3000000000 | bytes 3000000 | tf_op jit(solution)/shard_map/conv/pallas_call | solution.py:383
  30.1 4.7 %all-to-all-done.2.recv_ref = bf16[8,128,128]{2,1,0:T(8,128)(2,1)S(1)} async-done(((bf16[8,128,128]{2,1,0:T(8,128)(2,1)}), bf16[8,128,128]{2,1,0:T(8,128)(2,1)S(1)}, u32[]{:S(2)}, u32[]{:S(2)}) %all-to-all-start.2) | async-done | bytes 262176 | tf_op jit(solution)/shard_map/all_to_all | solution.py:378
  34.8 0.0 copy-start
  34.8 0.7 %copy-done = bf16[8,128,128]{2,1,0:T(8,128)(2,1)} copy-done((bf16[8,128,128]{2,1,0:T(8,128)(2,1)}, bf16[8,128,128]{2,1,0:T(8,128)(2,1)S(1)}, u32[]{:S(2)}) %copy-start) | copy-done | bytes 262168
  35.5 3.4 %grads.1 = f32[8,32,128]{2,1,0:T(8,128)} custom-call(bf16[8,128,128]{2,1,0:T(8,128)(2,1)} %copy-done, f32[256,1024]{1,0:T(8,128)} %get-tuple-element.11.spec_ref, bf16[64,2048]{1,0:T(8,128)(2,1)} %get-tuple-element.12.taps_ref, bf16[512,256]{1,0:T(8,128)(2,1)} %constant.14.clone.wf_ref, f32[128,16]{1,0:T(8,128)} %constant.16.clone.tw_ref), custom_call_target="tpu_custom_call" | custom-call | flops 1500000000 | bytes 3000000 | tf_op jit(solution)/shard_map/grads/pallas_call | solution.py:414
  38.9 0.0 copy-start.1
  38.9 11.5 %all_to_all.21.g_ref = f32[8,32,128]{2,1,0:T(8,128)} all-to-all(f32[8,32,128]{2,1,0:T(8,128)} %grads.1), channel_id=1, replica_groups=mesh['groups'=2,'ctx'=8,'mp'=2] {'ctx'}, dimensions={0} | all-to-all | bytes 262144 | tf_op jit(solution)/shard_map/all_to_all | solution.py:422
  50.4 0.0 copy-done.1
  50.4 11.3 %all_to_all.22.y_ref = bf16[8,128,128]{2,1,0:T(8,128)(2,1)} all-to-all(bf16[8,128,128]{2,1,0:T(8,128)(2,1)S(1)} %copy-done.1), channel_id=1, replica_groups=mesh['groups'=2,'ctx'=8,'mp'=2] {'ctx'}, dimensions={0} | all-to-all | bytes 524288 | tf_op jit(solution)/shard_map/all_to_all | solution.py:412
  61.6 1.8 %unpack.1 = (bf16[128,1024]{1,0:T(8,128)(2,1)}, f32[24,1024]{1,0:T(8,128)}, f32[3,1024]{1,0:T(4,128)}) custom-call(bf16[8,128,128]{2,1,0:T(8,128)(2,1)} %all_to_all.22.y_ref, f32[8,32,128]{2,1,0:T(8,128)} %all_to_all.21.g_ref), custom_call_target="tpu_custom_call" | custom-call | tf_op jit(solution)/shard_map/unpack/pallas_call | solution.py:424
Async XLA Ops:
  22.9 11.9 %all-to-all-start.2 = ((bf16[8,128,128]{2,1,0:T(8,128)(2,1)}), bf16[8,128,128]{2,1,0:T(8,128)(2,1)S(1)}, u32[]{:S(2)}, u32[]{:S(2)}) async-start(bf16[8,128,128]{2,1,0:T(8,128)(2,1)} %get-tuple-element.10), calls=%async_computation.2 | async-start | bytes 524288 | tf_op jit(solution)/shard_map/all_to_all | solution.py:378
  34.8 0.7 %copy-start = (bf16[8,128,128]{2,1,0:T(8,128)(2,1)}, bf16[8,128,128]{2,1,0:T(8,128)(2,1)S(1)}, u32[]{:S(2)}) copy-start(bf16[8,128,128]{2,1,0:T(8,128)(2,1)S(1)} %all-to-all-done.2.recv_ref) | copy-start | bytes 786436
  38.9 11.5 %copy-start.1 = (bf16[8,128,128]{2,1,0:T(8,128)(2,1)S(1)}, bf16[8,128,128]{2,1,0:T(8,128)(2,1)}, u32[]{:S(2)}) copy-start(bf16[8,128,128]{2,1,0:T(8,128)(2,1)} %get-tuple-element.9) | copy-start | bytes 786436

commit v2 on v1

--- a/solution.py
+++ b/solution.py
@@ -194,9 +194,9 @@
     return jnp.dot(a, b, preferred_element_type=f32)
 
 
-def outer_forward(src_ref, tw_ref, high_ref, low_ref, half, radix):
+def outer_forward(src_ref, start, tw_ref, high_ref, low_ref, half, radix):
     for r in range(0, radix, ROWS):
-        parts = half_forward([src_ref[h, r : r + ROWS, :].astype(f32) for h in range(half)])
+        parts = half_forward([src_ref[h, start + r : start + r + ROWS, :].astype(f32) for h in range(half)])
         for k, (re, im) in enumerate(parts):
             c, s = tw_ref[r : r + ROWS, k : k + 1], tw_ref[r : r + ROWS, half + k : half + k + 1]
             lanes = slice(k * LANES, (k + 1) * LANES)
@@ -212,19 +212,19 @@
     return first[:both] + first[both:] + dot(w_ref[:both, :], low_ref[:, lanes])
 
 
-def pack_kernel(x_ref, g_ref, f_ref, first_ref, second_ref, *, count):
+def pack_kernel(x_ref, g_ref, f_ref, send_ref):
     tok = x_ref.shape[0]
-    high, low = split_pair(f_ref[...].T)
+    high, low = split_pair(f_ref[...])
     taps = high.shape[0]
     pieces = jnp.concatenate([high.astype(f32), low.astype(f32)], axis=0).astype(bf16)
-    for j in range(count):
+    for j in range(send_ref.shape[0]):
         lanes = slice(j * LANES, (j + 1) * LANES)
-        first_ref[j, 0:tok, :] = x_ref[:, lanes]
-        first_ref[j, tok : tok + 2 * taps, :] = pieces
-        second_ref[j] = g_ref[:, lanes]
-
-
-def conv_kernel(
+        send_ref[j, 0:tok, :] = x_ref[:, lanes]
+        send_ref[j, tok : 2 * tok, :] = g_ref[:, lanes]
+        send_ref[j, 2 * tok : 2 * tok + 2 * taps, :] = pieces
+
+
+def main_kernel(
     place_ref,
     recv_ref,
     mix_ref,
@@ -233,13 +233,15 @@
     wi_ref,
     tw_ref,
     twt_ref,
-    y_ref,
-    spec_ref,
-    taps_ref,
+    out_ref,
     a_high,
     a_low,
     b_high,
     b_low,
+    spec_ref,
+    taps_ref,
+    p_high,
+    p_low,
     *,
     half,
     radix,
@@ -248,9 +250,10 @@
     taps = mix_ref.shape[0]
     order = ar_ref.shape[0]
     width = 2 * radix
+    scale = 1.0 / (half * radix)
     blocks = []
     for h in range(half):
-        both = recv_ref[h, radix : radix + 2 * taps, :].astype(f32)
+        both = recv_ref[h, 2 * radix : 2 * radix + 2 * taps, :].astype(f32)
         value = both[:taps] + both[taps:]
         extra = jnp.zeros((kp - taps, radix), f32)
         if h == 0:
@@ -276,9 +279,10 @@
         lanes = slice(k * width, (k + 1) * width)
         taps_ref[0:kp, lanes] = f_high[rows]
         taps_ref[kp : 2 * kp, lanes] = f_low[rows]
-    weights = jnp.concatenate(
-        [mix_ref[...], ar_ref[...], jnp.zeros((kp - taps - order, LANES), f32)], axis=0
-    ) * (1.0 / (half * radix))
+    weights = (
+        jnp.concatenate([mix_ref[...], ar_ref[...], jnp.zeros((kp - taps - order, LANES), f32)], axis=0)
+        * scale
+    )
     m_high, m_low = split_pair(weights)
     zero = jnp.zeros_like(m_high)
 
@@ -290,7 +294,7 @@
     d_high, d_low = diagonal(m_high), diagonal(m_low)
     mixer = jnp.concatenate([d_high, d_high, d_low], axis=0)
 
-    outer_forward(recv_ref, tw_ref, b_high, b_low, half, radix)
+    outer_forward(recv_ref, 0, tw_ref, b_high, b_low, half, radix)
     for m in range(half // 2):
         lanes = slice(m * 2 * LANES, (m + 1) * 2 * LANES)
         rows = slice(2 * m * kp, 2 * (m + 1) * kp)
@@ -320,11 +324,9 @@
             c, s = tw_ref[r : r + ROWS, k : k + 1], tw_ref[r : r + ROWS, half + k : half + k + 1]
             us.append((gr * c - gi * s, gr * s + gi * c))
         for h, value in enumerate(half_inverse(us)):
-            y_ref[h, r : r + ROWS, :] = value.astype(bf16)
-
-
-def grad_kernel(recv_ref, spec_ref, taps_ref, wf_ref, tw_ref, out_ref, b_high, b_low, p_high, p_low, *, half, radix, kp):
-    outer_forward(recv_ref, tw_ref, b_high, b_low, half, radix)
+            out_ref[h, r : r + ROWS, :] = value.astype(bf16)
+
+    outer_forward(recv_ref, radix, tw_ref, b_high, b_low, half, radix)
     for m in range(half // 2):
         lanes = slice(m * 2 * LANES, (m + 1) * 2 * LANES)
         cot = inner_dft(wf_ref, b_high, b_low, lanes)
@@ -338,18 +340,29 @@
                 p_high[row : row + radix, :] = high[:, part]
                 p_low[row : row + radix, :] = low[:, part]
     first = dot(taps_ref[...], p_high[...])
-    grads = (first[:kp] + first[kp:] + dot(taps_ref[0:kp, :], p_low[...])) * (1.0 / (half * radix))
+    grads = (first[:kp] + first[kp:] + dot(taps_ref[0:kp, :], p_low[...])) * scale
+    g_high, g_low = split_pair(grads)
+    used = taps + order
+    fill = out_ref.shape[1] - radix - 2 * used
+    pieces = [g_high.astype(f32)[:used], g_low.astype(f32)[:used]]
+    if fill:
+        pieces.append(jnp.zeros((fill, LANES), f32))
+    pieces = jnp.concatenate(pieces, axis=0).astype(bf16)
     for j in range(out_ref.shape[0]):
-        out_ref[j] = grads
-
-
-def unpack_kernel(y_ref, g_ref, out_ref, mix_ref, ar_ref, *, count):
+        out_ref[j, radix:, :] = pieces
+
+
+def unpack_kernel(back_ref, out_ref, mix_ref, ar_ref):
+    tok = out_ref.shape[0]
     taps, order = mix_ref.shape[0], ar_ref.shape[0]
-    for j in range(count):
+    used = taps + order
+    for j in range(back_ref.shape[0]):
         lanes = slice(j * LANES, (j + 1) * LANES)
-        out_ref[:, lanes] = y_ref[j]
-        mix_ref[:, lanes] = g_ref[j, 0:taps, :]
-        ar_ref[:, lanes] = g_ref[j, taps : taps + order, :]
+        out_ref[:, lanes] = back_ref[j, 0:tok, :]
+        pieces = back_ref[j, tok:, :].astype(f32)
+        grads = pieces[0:used] + pieces[used : 2 * used]
+        mix_ref[:, lanes] = grads[0:taps]
+        ar_ref[:, lanes] = grads[taps:used]
 
 
 def shape_of(*dims, dtype=f32):
@@ -363,30 +376,27 @@
     half, radix = count, tok_rows
     kp = -(-(taps + order) // 8) * 8
     wf, wi, twist, twist_t = dft_constants(half, radix)
-    rows = tok_rows + 2 * taps
-
-    first, second = pl.pallas_call(
-        functools.partial(pack_kernel, count=count),
-        out_shape=(
-            shape_of(count, rows, LANES, dtype=bf16),
-            shape_of(count, tok_rows, LANES, dtype=bf16),
-        ),
+    rows = 2 * tok_rows + 2 * taps
+    back_rows = -(-(tok_rows + 2 * (taps + order)) // 8) * 8
+    swap = functools.partial(lax.all_to_all, axis_name="ctx", split_axis=0, concat_axis=0, tiled=True)
+    small = pltpu.CompilerParams(vmem_limit_bytes=8 << 20)
+
+    send = pl.pallas_call(
+        pack_kernel,
+        out_shape=shape_of(count, rows, LANES, dtype=bf16),
+        compiler_params=small,
         name="pack",
-    )(inputs, cotangent, filters)
-    swap = functools.partial(lax.all_to_all, axis_name="ctx", split_axis=0, concat_axis=0, tiled=True)
-    first = swap(first)
-    second = swap(second)
+    )(inputs, cotangent, filters.T)
+    recv = swap(send)
 
     whole = lambda *dims: pl.BlockSpec(dims, lambda i, place: (0,) * len(dims))
     place = lax.axis_index("ctx").astype(jnp.int32).reshape(1)
     span = half * LANES
-    y_cols, spec, spectra = pl.pallas_call(
-        functools.partial(conv_kernel, half=half, radix=radix, kp=kp),
-        out_shape=(
-            shape_of(count, tok_rows, LANES, dtype=bf16),
-            shape_of(2 * radix, span),
-            shape_of(2 * kp, half * 2 * radix, dtype=bf16),
-        ),
+    split = pltpu.VMEM((2 * radix, span), bf16)
+    tall = pltpu.VMEM((half * 2 * radix, LANES), bf16)
+    result = pl.pallas_call(
+        functools.partial(main_kernel, half=half, radix=radix, kp=kp),
+        out_shape=shape_of(count, back_rows, LANES, dtype=bf16),
         grid_spec=pltpu.PrefetchScalarGridSpec(
             num_scalar_prefetch=1,
             grid=(1,),
@@ -399,37 +409,26 @@
                 whole(*twist.shape),
                 whole(*twist_t.shape),
             ],
-            out_specs=(
-                whole(count, tok_rows, LANES),
-                whole(2 * radix, span),
-                whole(2 * kp, half * 2 * radix),
-            ),
-            scratch_shapes=[pltpu.VMEM((2 * radix, span), bf16)] * 4,
+            out_specs=whole(count, back_rows, LANES),
+            scratch_shapes=[split] * 4
+            + [pltpu.VMEM((2 * radix, span), f32), pltpu.VMEM((2 * kp, half * 2 * radix), bf16)]
+            + [tall] * 2,
         ),
-        cost_estimate=pl.CostEstimate(flops=3_000_000_000, bytes_accessed=3_000_000, transcendentals=0),
-        name="conv",
-    )(place, first, mixing, ar_coef, wf, wi, twist, twist_t)
-    y_rows = swap(y_cols)
-
-    grads = pl.pallas_call(
-        functools.partial(grad_kernel, half=half, radix=radix, kp=kp),
-        out_shape=shape_of(count, kp, LANES),
-        scratch_shapes=[pltpu.VMEM((2 * radix, span), bf16)] * 2
-        + [pltpu.VMEM((half * 2 * radix, LANES), bf16)] * 2,
-        cost_estimate=pl.CostEstimate(flops=1_500_000_000, bytes_accessed=3_000_000, transcendentals=0),
-        name="grads",
-    )(second, spec, spectra, wf, twist)
-    grads = swap(grads)
+        compiler_params=pltpu.CompilerParams(vmem_limit_bytes=24 << 20),
+        name="main",
+    )(place, recv, mixing, ar_coef, wf, wi, twist, twist_t)
+    back = swap(result)
 
     return pl.pallas_call(
-        functools.partial(unpack_kernel, count=count),
+        unpack_kernel,
         out_shape=(
             shape_of(tok_rows, local_width, dtype=bf16),
             shape_of(taps, local_width),
             shape_of(order, local_width),
         ),
+        compiler_params=small,
         name="unpack",
-    )(y_rows, grads)
+    )(back)
 
 
 def local(inputs, cotangent, filters, mixing, ar_coef):
@@ -438,7 +437,7 @@
     tiled = (
         local_width == count * LANES
         and tok_rows == LANES
-        and count in (2, 4, 8, 16)
+        and count in (2, 4, 8)
         and filters.shape[1] % 8 == 0
     )
     return (local_tiled if tiled else local_general)(inputs, cotangent, filters, mixing, ar_coef)

time: 64 us -> 47.8 us (0.75)
  blocking collectives: 41.6 us -> 15.4 us
  waiting for transfers between devices: 4.66 us -> 16.6 us
  Pallas kernels: 11 us -> 4.71 us
  starting transfers between devices: 3.41 us -> 7.42 us
    all_to_all x3 -> x1, blocking collectives: 41.6 us -> 15.4 us  [local_tiled(): back = swap(result)]
    all_to_all x1, waiting for transfers between devices: 4.66 us -> 16.6 us  [local_tiled(): recv = swap(send)]
    pallas_call x4 -> x3, Pallas kernels: 11 us -> 4.71 us  [the longest x1 2.98 us: local_tiled(): pl.pallas_call(functools.partial(main_kernel, half=half, radix=radix, kp=...]
    all_to_all x1, starting transfers between devices: 3.41 us -> 7.42 us  [local_tiled(): recv = swap(send)]
    unnamed x5 -> x18, local copies, waits for them, and re-layouts: 2.14 us -> 2.62 us
  transfers between devices with their start and end apart: 1 -> 1, of which waited for: 1 -> 1; matrix products, arithmetic and copies ran while one was open for 0% -> 0% of each run, Pallas kernels for 6% -> 0%
where the time goes in v2:
time: 47.8 us; the launch traced here: 47.4 us
  waiting for transfers between devices  16.6 us (35%)
  blocking collectives  15.4 us (32%)
  starting transfers between devices  7.42 us (16%)
  Pallas kernels  4.71 us (10%)
  local copies, waits for them, and re-layouts  2.62 us (5%)
  between operations  0.7 us (1%)
    all_to_all x1, waiting for transfers between devices, local_tiled(): recv = swap(send)  16.6 us
    all_to_all x1, blocking collectives, local_tiled(): back = swap(result)  15.4 us
    all_to_all x1, starting transfers between devices, local_tiled(): recv = swap(send)  7.42 us
    pallas_call x1, Pallas kernels, local_tiled(): pl.pallas_call(functools.partial(main_kernel, half=half, radix=radix, kp=...  2.98 us
    unnamed x18, local copies, waits for them, and re-layouts  2.62 us
  transfers between devices with their start and end apart: 1, of which 1 were waited for; matrix products, arithmetic and copies ran while one was open for 0% of the time, Pallas kernels for 0%

profile of v2, /device:TPU:0, one launch (start us, length us, event | category | flops | bytes accessed | tf_op | source)
XLA Modules:
  0.0 47.4 jit_solution(14290590735091509189)
XLA Ops:
  0.6 0.0 copy-start.2
  0.6 0.9 %copy-done.2 = bf16[128,1024]{1,0:T(8,128)(2,1)S(1)} copy-done((bf16[128,1024]{1,0:T(8,128)(2,1)S(1)}, bf16[128,1024]{1,0:T(8,128)(2,1)}, u32[]{:S(2)}) %copy-start.2) | copy-done | bytes 262168
  1.6 0.0 copy-start.3
  1.6 0.9 %copy-done.3 = bf16[128,1024]{1,0:T(8,128)(2,1)S(1)} copy-done((bf16[128,1024]{1,0:T(8,128)(2,1)S(1)}, bf16[128,1024]{1,0:T(8,128)(2,1)}, u32[]{:S(2)}) %copy-start.3) | copy-done | bytes 262168
  2.5 0.0 copy-start.7
  2.5 0.7 %copy-done.7 = f32[128,24]{0,1:T(8,128)S(1)} copy-done((f32[128,24]{0,1:T(8,128)S(1)}, f32[128,24]{0,1:T(8,128)}, u32[]{:S(2)}) %copy-start.7) | copy-done | bytes 12312
  3.2 0.9 %pack.1 = bf16[8,304,128]{2,1,0:T(8,128)(2,1)} custom-call(bf16[128,1024]{1,0:T(8,128)(2,1)S(1)} %copy-done.2, bf16[128,1024]{1,0:T(8,128)(2,1)S(1)} %copy-done.3, f32[24,128]{1,0:T(8,128)S(1)} %bitcast.2), custom_call_target="tpu_custom_call" | custom-call | tf_op jit(solution)/shard_map/pack/pallas_call | solution.py:384
  4.2 0.0 copy-start
  4.2 0.0 copy-start.1
  4.2 0.0 copy-start.4
  4.2 0.0 copy-start.5
  4.2 0.0 copy-start.6
  4.2 7.4 %all-to-all-start = ((bf16[8,304,128]{2,1,0:T(8,128)(2,1)}), bf16[8,304,128]{2,1,0:T(8,128)(2,1)S(1)}, u32[]{:S(2)}, u32[]{:S(2)}) async-start(bf16[8,304,128]{2,1,0:T(8,128)(2,1)} %pack.1), calls=%async_computation | async-start | bytes 1245184 | tf_op jit(solution)/shard_map/all_to_all | solution.py:390
  11.6 0.0 copy-start.8
  11.6 16.6 %all-to-all-done.recv_ref = bf16[8,304,128]{2,1,0:T(8,128)(2,1)S(1)} async-done(((bf16[8,304,128]{2,1,0:T(8,128)(2,1)}), bf16[8,304,128]{2,1,0:T(8,128)(2,1)S(1)}, u32[]{:S(2)}, u32[]{:S(2)}) %all-to-all-start) | async-done | bytes 622624 | tf_op jit(solution)/shard_map/all_to_all | solution.py:390
  28.2 0.0 copy-done
  28.2 0.0 copy-done.1
  28.2 0.0 copy-done.4
  28.2 0.0 copy-done.5
  28.2 0.0 copy-done.6
  28.2 0.0 copy-done.8
  28.2 3.0 %main.1 = bf16[8,184,128]{2,1,0:T(8,128)(2,1)S(1)} custom-call(s32[1]{0:T(128)} %bitcast.place_ref, bf16[8,304,128]{2,1,0:T(8,128)(2,1)S(1)} %all-to-all-done.recv_ref, f32[24,1024]{1,0:T(8,128)S(1)} %copy-done.4, f32[3,1024]{1,0:T(4,128)S(1)} %copy-done.6, bf16[512,256]{1,0:T(8,128)(2,1)S(1)} %copy-done, bf16[512,256]{1,0:T(8,128)(2,1)S(1)} %copy-done.1, ...), custom_call_target="tpu_custom_call" | custom-call | tf_op jit(solution)/shard_map/main/pallas_call | solution.py:397
  31.2 15.4 %all_to_all.10.back_ref = bf16[8,184,128]{2,1,0:T(8,128)(2,1)S(1)} all-to-all(bf16[8,184,128]{2,1,0:T(8,128)(2,1)S(1)} %main.1), channel_id=1, replica_groups=mesh['groups'=2,'ctx'=8,'mp'=2] {'ctx'}, dimensions={0} | all-to-all | bytes 753664 | tf_op jit(solution)/shard_map/all_to_all | solution.py:420
  46.6 0.8 %unpack.1 = (bf16[128,1024]{1,0:T(8,128)(2,1)}, f32[24,1024]{1,0:T(8,128)}, f32[3,1024]{1,0:T(4,128)}) custom-call(bf16[8,184,128]{2,1,0:T(8,128)(2,1)S(1)} %all_to_all.10.back_ref), custom_call_target="tpu_custom_call" | custom-call | tf_op jit(solution)/shard_map/unpack/pallas_call | solution.py:422
Async XLA Ops:
  0.6 1.0 %copy-start.2 = (bf16[128,1024]{1,0:T(8,128)(2,1)S(1)}, bf16[128,1024]{1,0:T(8,128)(2,1)}, u32[]{:S(2)}) copy-start(bf16[128,1024]{1,0:T(8,128)(2,1)} %x_ref.1) | copy-start | bytes 786436
  1.6 0.9 %copy-start.3 = (bf16[128,1024]{1,0:T(8,128)(2,1)S(1)}, bf16[128,1024]{1,0:T(8,128)(2,1)}, u32[]{:S(2)}) copy-start(bf16[128,1024]{1,0:T(8,128)(2,1)} %g_ref.1) | copy-start | bytes 786436
  2.5 0.7 %copy-start.7 = (f32[128,24]{0,1:T(8,128)S(1)}, f32[128,24]{0,1:T(8,128)}, u32[]{:S(2)}) copy-start(f32[128,24]{0,1:T(8,128)} %param.11) | copy-start | bytes 36868
  4.2 24.0 %copy-start = (bf16[512,256]{1,0:T(8,128)(2,1)S(1)}, bf16[512,256]{1,0:T(8,128)(2,1)}, u32[]{:S(2)}) copy-start(bf16[512,256]{1,0:T(8,128)(2,1)} %constant.14.clone.wf_ref) | copy-start | bytes 786436
  4.2 24.0 %copy-start.1 = (bf16[512,256]{1,0:T(8,128)(2,1)S(1)}, bf16[512,256]{1,0:T(8,128)(2,1)}, u32[]{:S(2)}) copy-start(bf16[512,256]{1,0:T(8,128)(2,1)} %constant.15.clone.wi_ref) | copy-start | bytes 786436
  4.2 24.0 %copy-start.4 = (f32[24,1024]{1,0:T(8,128)S(1)}, f32[24,1024]{1,0:T(8,128)}, u32[]{:S(2)}) copy-start(f32[24,1024]{1,0:T(8,128)} %mix_ref.1) | copy-start | bytes 294916
  4.2 24.0 %copy-start.5 = (f32[128,16]{1,0:T(8,128)S(1)}, f32[128,16]{1,0:T(8,128)}, u32[]{:S(2)}) copy-start(f32[128,16]{1,0:T(8,128)} %constant.16.clone.tw_ref) | copy-start | bytes 24580
  4.2 24.1 %copy-start.6 = (f32[3,1024]{1,0:T(4,128)S(1)}, f32[3,1024]{1,0:T(4,128)}, u32[]{:S(2)}) copy-start(f32[3,1024]{1,0:T(4,128)} %ar_ref.1) | copy-start | bytes 36868
  4.2 24.0 %all-to-all-start = ((bf16[8,304,128]{2,1,0:T(8,128)(2,1)}), bf16[8,304,128]{2,1,0:T(8,128)(2,1)S(1)}, u32[]{:S(2)}, u32[]{:S(2)}) async-start(bf16[8,304,128]{2,1,0:T(8,128)(2,1)} %pack.1), calls=%async_computation | async-start | bytes 1245184 | tf_op jit(solution)/shard_map/all_to_all | solution.py:390
  11.6 16.6 %copy-start.8 = (f32[16,128]{1,0:T(8,128)S(1)}, f32[16,128]{1,0:T(8,128)}, u32[]{:S(2)}) copy-start(f32[16,128]{1,0:T(8,128)} %constant.17.clone.twt_ref) | copy-start | bytes 24580

commit v3 on v2

--- a/solution.py
+++ b/solution.py
@@ -212,16 +212,34 @@
     return first[:both] + first[both:] + dot(w_ref[:both, :], low_ref[:, lanes])
 
 
-def pack_kernel(x_ref, g_ref, f_ref, send_ref):
+def pack_kernel(x_ref, g_ref, f_ref, send_ref, buf, in_sem, out_sem):
+    count, rows, _ = send_ref.shape
     tok = x_ref.shape[0]
+    copies = []
+    for j in range(count):
+        lanes = pl.ds(j * LANES, LANES)
+        for side, src in enumerate((x_ref, g_ref)):
+            copy = pltpu.make_async_copy(
+                src.at[:, lanes], buf.at[j, pl.ds(side * tok, tok), :], in_sem.at[2 * j + side]
+            )
+            copy.start()
+            copies.append(copy)
+    @pl.when(lax.axis_index("mp") == 0)
+    def _():
+        pl.delay(5500)
+
     high, low = split_pair(f_ref[...])
-    taps = high.shape[0]
     pieces = jnp.concatenate([high.astype(f32), low.astype(f32)], axis=0).astype(bf16)
-    for j in range(send_ref.shape[0]):
-        lanes = slice(j * LANES, (j + 1) * LANES)
-        send_ref[j, 0:tok, :] = x_ref[:, lanes]
-        send_ref[j, tok : 2 * tok, :] = g_ref[:, lanes]
-        send_ref[j, 2 * tok : 2 * tok + 2 * taps, :] = pieces
+    sends = []
+    for j in range(count):
+        buf[j, 2 * tok :, :] = pieces
+        copies[2 * j].wait()
+        copies[2 * j + 1].wait()
+        send = pltpu.make_async_copy(buf.at[j], send_ref.at[j], out_sem.at[j])
+        send.start()
+        sends.append(send)
+    for send in sends:
+        send.wait()
 
 
 def main_kernel(
@@ -384,7 +402,17 @@
     send = pl.pallas_call(
         pack_kernel,
         out_shape=shape_of(count, rows, LANES, dtype=bf16),
-        compiler_params=small,
+        in_specs=[
+            pl.BlockSpec(memory_space=pl.ANY),
+            pl.BlockSpec(memory_space=pl.ANY),
+            pl.BlockSpec(memory_space=pltpu.VMEM),
+        ],
+        out_specs=pl.BlockSpec(memory_space=pl.ANY),
+        scratch_shapes=[
+            pltpu.VMEM((count, rows, LANES), bf16),
+            pltpu.SemaphoreType.DMA((2 * count,)),
+            pltpu.SemaphoreType.DMA((count,)),
+        ],
         name="pack",
     )(inputs, cotangent, filters.T)
     recv = swap(send)

time: 47.8 us -> 44.3 us (0.927)
  Pallas kernels: 4.71 us -> 11.1 us
  waiting for transfers between devices: 16.6 us -> 11.9 us
  local copies, waits for them, and re-layouts: 2.62 us -> 0.04 us
  blocking collectives: 15.4 us -> 12.9 us
    pallas_call x1, Pallas kernels: 0.92 us -> 7.26 us  [local_tiled(): pl.pallas_call(pack_kernel, out_shape=shape_of(count, rows, LANES, dtype=...]
    all_to_all x1, waiting for transfers between devices: 16.6 us -> 11.9 us  [local_tiled(): recv = swap(send)]
    unnamed x18 -> x12, local copies, waits for them, and re-layouts: 2.62 us -> 0.04 us
    all_to_all x1, blocking collectives: 15.4 us -> 12.9 us  [local_tiled(): back = swap(result)]
where the time goes in v3:
time: 44.3 us; the launch traced here: 44 us
  blocking collectives  12.9 us (29%)
  waiting for transfers between devices  11.9 us (27%)
  Pallas kernels  11.1 us (25%)
  starting transfers between devices  7.42 us (17%)
  between operations  0.72 us (2%)
    all_to_all x1, blocking collectives, local_tiled(): back = swap(result)  12.9 us
    all_to_all x1, waiting for transfers between devices, local_tiled(): recv = swap(send)  11.9 us
    all_to_all x1, starting transfers between devices, local_tiled(): recv = swap(send)  7.42 us
    pallas_call x1, Pallas kernels, local_tiled(): pl.pallas_call(pack_kernel, out_shape=shape_of(count, rows, LANES, dtype=...  7.26 us
    pallas_call x1, Pallas kernels, local_tiled(): pl.pallas_call(functools.partial(main_kernel, half=half, radix=radix, kp=...  2.97 us
  transfers between devices with their start and end apart: 1, of which 1 were waited for; matrix products, arithmetic and copies ran while one was open for 0% of the time, Pallas kernels for 0%

profile of v3, /device:TPU:0, one launch (start us, length us, event | category | flops | bytes accessed | tf_op | source)
XLA Modules:
  0.0 44.0 jit_solution(2011590237141079158)
XLA Ops:
  0.6 7.3 %pack.1 = bf16[8,304,128]{2,1,0:T(8,128)(2,1)} custom-call(bf16[128,1024]{1,0:T(8,128)(2,1)} %x_ref.1, bf16[128,1024]{1,0:T(8,128)(2,1)} %g_ref.1, f32[24,128]{1,0:T(8,128)} %bitcast.2), custom_call_target="tpu_custom_call" | custom-call | tf_op jit(solution)/shard_map/pack/pallas_call | solution.py:402
  7.9 0.0 copy-start
  7.9 0.0 copy-start.1
  7.9 0.0 copy-start.2
  7.9 0.0 copy-start.3
  8.0 0.0 copy-start.4
  8.0 7.4 %all-to-all-start = ((bf16[8,304,128]{2,1,0:T(8,128)(2,1)}), bf16[8,304,128]{2,1,0:T(8,128)(2,1)S(1)}, u32[]{:S(2)}, u32[]{:S(2)}) async-start(bf16[8,304,128]{2,1,0:T(8,128)(2,1)} %pack.1), calls=%async_computation | async-start | bytes 1245184 | tf_op jit(solution)/shard_map/all_to_all | solution.py:418
  15.4 0.0 copy-start.5
  15.4 11.9 %all-to-all-done.recv_ref = bf16[8,304,128]{2,1,0:T(8,128)(2,1)S(1)} async-done(((bf16[8,304,128]{2,1,0:T(8,128)(2,1)}), bf16[8,304,128]{2,1,0:T(8,128)(2,1)S(1)}, u32[]{:S(2)}, u32[]{:S(2)}) %all-to-all-start) | async-done | bytes 622624 | tf_op jit(solution)/shard_map/all_to_all | solution.py:418
  27.3 0.0 copy-done
  27.3 0.0 copy-done.1
  27.3 0.0 copy-done.2
  27.3 0.0 copy-done.3
  27.3 0.0 copy-done.4
  27.3 0.0 copy-done.5
  27.3 3.0 %main.1 = bf16[8,184,128]{2,1,0:T(8,128)(2,1)S(1)} custom-call(s32[1]{0:T(128)} %bitcast.place_ref, bf16[8,304,128]{2,1,0:T(8,128)(2,1)S(1)} %all-to-all-done.recv_ref, f32[24,1024]{1,0:T(8,128)S(1)} %copy-done.2, f32[3,1024]{1,0:T(4,128)S(1)} %copy-done.4, bf16[512,256]{1,0:T(8,128)(2,1)S(1)} %copy-done, bf16[512,256]{1,0:T(8,128)(2,1)S(1)} %copy-done.1, ...), custom_call_target="tpu_custom_call" | custom-call | tf_op jit(solution)/shard_map/main/pallas_call | solution.py:425
  30.3 12.9 %all_to_all.10.back_ref = bf16[8,184,128]{2,1,0:T(8,128)(2,1)S(1)} all-to-all(bf16[8,184,128]{2,1,0:T(8,128)(2,1)S(1)} %main.1), channel_id=1, replica_groups=mesh['groups'=2,'ctx'=8,'mp'=2] {'ctx'}, dimensions={0} | all-to-all | bytes 753664 | tf_op jit(solution)/shard_map/all_to_all | solution.py:448
  43.2 0.8 %unpack.1 = (bf16[128,1024]{1,0:T(8,128)(2,1)}, f32[24,1024]{1,0:T(8,128)}, f32[3,1024]{1,0:T(4,128)}) custom-call(bf16[8,184,128]{2,1,0:T(8,128)(2,1)S(1)} %all_to_all.10.back_ref), custom_call_target="tpu_custom_call" | custom-call | tf_op jit(solution)/shard_map/unpack/pallas_call | solution.py:450
Async XLA Ops:
  7.9 19.4 %copy-start = (bf16[512,256]{1,0:T(8,128)(2,1)S(1)}, bf16[512,256]{1,0:T(8,128)(2,1)}, u32[]{:S(2)}) copy-start(bf16[512,256]{1,0:T(8,128)(2,1)} %constant.14.clone.wf_ref) | copy-start | bytes 786436
  7.9 19.4 %copy-start.1 = (bf16[512,256]{1,0:T(8,128)(2,1)S(1)}, bf16[512,256]{1,0:T(8,128)(2,1)}, u32[]{:S(2)}) copy-start(bf16[512,256]{1,0:T(8,128)(2,1)} %constant.15.clone.wi_ref) | copy-start | bytes 786436
  7.9 19.4 %copy-start.2 = (f32[24,1024]{1,0:T(8,128)S(1)}, f32[24,1024]{1,0:T(8,128)}, u32[]{:S(2)}) copy-start(f32[24,1024]{1,0:T(8,128)} %mix_ref.1) | copy-start | bytes 294916
  7.9 19.3 %copy-start.3 = (f32[128,16]{1,0:T(8,128)S(1)}, f32[128,16]{1,0:T(8,128)}, u32[]{:S(2)}) copy-start(f32[128,16]{1,0:T(8,128)} %constant.16.clone.tw_ref) | copy-start | bytes 24580
  8.0 19.3 %copy-start.4 = (f32[3,1024]{1,0:T(4,128)S(1)}, f32[3,1024]{1,0:T(4,128)}, u32[]{:S(2)}) copy-start(f32[3,1024]{1,0:T(4,128)} %ar_ref.1) | copy-start | bytes 36868
  8.0 19.3 %all-to-all-start = ((bf16[8,304,128]{2,1,0:T(8,128)(2,1)}), bf16[8,304,128]{2,1,0:T(8,128)(2,1)S(1)}, u32[]{:S(2)}, u32[]{:S(2)}) async-start(bf16[8,304,128]{2,1,0:T(8,128)(2,1)} %pack.1), calls=%async_computation | async-start | bytes 1245184 | tf_op jit(solution)/shard_map/all_to_all | solution.py:418
  15.4 11.9 %copy-start.5 = (f32[16,128]{1,0:T(8,128)S(1)}, f32[16,128]{1,0:T(8,128)}, u32[]{:S(2)}) copy-start(f32[16,128]{1,0:T(8,128)} %constant.17.clone.twt_ref) | copy-start | bytes 24580

commit v4 on v3

--- a/solution.py
+++ b/solution.py
@@ -12,6 +12,7 @@
 ORDER = 3
 LANES = 128
 ROWS = 16
+STAGGER_NS = 5500
 
 f32 = jnp.float32
 bf16 = jnp.bfloat16
@@ -187,7 +188,10 @@
 
     theta = 2.0 * np.pi * index[:, None] * (np.arange(half)[None, :] + 0.5) / (2 * half * radix)
     twist = np.concatenate([np.cos(theta), np.sin(theta)], axis=1).astype(np.float32)
-    return stacked(forward), stacked(forward.T), twist, np.ascontiguousarray(twist.T)
+    table = np.zeros((radix + 2 * half, radix), np.float32)
+    table[:radix, : 2 * half] = twist
+    table[radix:] = twist.T
+    return stacked(forward), stacked(forward.T), table
 
 
 def dot(a, b):
@@ -212,9 +216,11 @@
     return first[:both] + first[both:] + dot(w_ref[:both, :], low_ref[:, lanes])
 
 
-def pack_kernel(x_ref, g_ref, f_ref, send_ref, buf, in_sem, out_sem):
+def pack_kernel(x_ref, g_ref, f_ref, send_ref, buf, fbuf, in_sem, out_sem, *, wait):
     count, rows, _ = send_ref.shape
     tok = x_ref.shape[0]
+    taps_in = pltpu.make_async_copy(f_ref, fbuf, in_sem.at[2 * count])
+    taps_in.start()
     copies = []
     for j in range(count):
         lanes = pl.ds(j * LANES, LANES)
@@ -224,15 +230,18 @@
             )
             copy.start()
             copies.append(copy)
+
     @pl.when(lax.axis_index("mp") == 0)
     def _():
-        pl.delay(5500)
-
-    high, low = split_pair(f_ref[...])
+        pl.delay(wait)
+
+    taps_in.wait()
+    high, low = split_pair(fbuf[...])
     pieces = jnp.concatenate([high.astype(f32), low.astype(f32)], axis=0).astype(bf16)
+    for j in range(count):
+        buf[j, 2 * tok :, :] = pieces
     sends = []
     for j in range(count):
-        buf[j, 2 * tok :, :] = pieces
         copies[2 * j].wait()
         copies[2 * j + 1].wait()
         send = pltpu.make_async_copy(buf.at[j], send_ref.at[j], out_sem.at[j])
@@ -250,7 +259,6 @@
     wf_ref,
     wi_ref,
     tw_ref,
-    twt_ref,
     out_ref,
     a_high,
     a_low,
@@ -280,7 +288,7 @@
             extra = jnp.where((row < order) & (lane == row + 1), 1.0, extra)
         blocks.append(jnp.concatenate([value, extra], axis=0))
     for k, (re, im) in enumerate(half_forward(blocks)):
-        c, s = twt_ref[k : k + 1, :], twt_ref[half + k : half + k + 1, :]
+        c, s = tw_ref[radix + k : radix + k + 1, :], tw_ref[radix + half + k : radix + half + k + 1, :]
         value = jnp.concatenate([re * c + im * s, im * c - re * s], axis=1)
         high, low = split_pair(value)
         a_high[k * kp : (k + 1) * kp, 0:width] = high
@@ -393,24 +401,21 @@
     taps, order = filters.shape[1], ar_coef.shape[0]
     half, radix = count, tok_rows
     kp = -(-(taps + order) // 8) * 8
-    wf, wi, twist, twist_t = dft_constants(half, radix)
+    wf, wi, twist = dft_constants(half, radix)
     rows = 2 * tok_rows + 2 * taps
     back_rows = -(-(tok_rows + 2 * (taps + order)) // 8) * 8
     swap = functools.partial(lax.all_to_all, axis_name="ctx", split_axis=0, concat_axis=0, tiled=True)
     small = pltpu.CompilerParams(vmem_limit_bytes=8 << 20)
 
     send = pl.pallas_call(
-        pack_kernel,
+        functools.partial(pack_kernel, wait=STAGGER_NS),
         out_shape=shape_of(count, rows, LANES, dtype=bf16),
-        in_specs=[
-            pl.BlockSpec(memory_space=pl.ANY),
-            pl.BlockSpec(memory_space=pl.ANY),
-            pl.BlockSpec(memory_space=pltpu.VMEM),
-        ],
+        in_specs=[pl.BlockSpec(memory_space=pl.ANY)] * 3,
         out_specs=pl.BlockSpec(memory_space=pl.ANY),
         scratch_shapes=[
             pltpu.VMEM((count, rows, LANES), bf16),
-            pltpu.SemaphoreType.DMA((2 * count,)),
+            pltpu.VMEM((taps, tok_rows), f32),
+            pltpu.SemaphoreType.DMA((2 * count + 1,)),
             pltpu.SemaphoreType.DMA((count,)),
         ],
         name="pack",
@@ -435,7 +440,6 @@
                 whole(*wf.shape),
                 whole(*wi.shape),
                 whole(*twist.shape),
-                whole(*twist_t.shape),
             ],
             out_specs=whole(count, back_rows, LANES),
             scratch_shapes=[split] * 4
@@ -444,7 +448,7 @@
         ),
         compiler_params=pltpu.CompilerParams(vmem_limit_bytes=24 << 20),
         name="main",
-    )(place, recv, mixing, ar_coef, wf, wi, twist, twist_t)
+    )(place, recv, mixing, ar_coef, wf, wi, twist)
     back = swap(result)
 
     return pl.pallas_call(

time: 44.3 us -> 43.6 us (0.984)
  Pallas kernels: 11.1 us -> 10.4 us
    pallas_call x1, Pallas kernels: 7.26 us -> 6.61 us  [local_tiled(): pl.pallas_call(functools.partial(pack_kernel, wait=STAGGER_NS), out_shape...]
where the time goes in v4:
time: 43.6 us; the launch traced here: 43.3 us
  blocking collectives  12.9 us (30%)
  waiting for transfers between devices  11.9 us (27%)
  Pallas kernels  10.4 us (24%)
  starting transfers between devices  7.42 us (17%)
  between operations  0.71 us (2%)
    all_to_all x1, blocking collectives, local_tiled(): back = swap(result)  12.9 us
    all_to_all x1, waiting for transfers between devices, local_tiled(): recv = swap(send)  11.9 us
    all_to_all x1, starting transfers between devices, local_tiled(): recv = swap(send)  7.42 us
    pallas_call x1, Pallas kernels, local_tiled(): pl.pallas_call(functools.partial(pack_kernel, wait=STAGGER_NS), out_shape...  6.61 us
    pallas_call x1, Pallas kernels, local_tiled(): pl.pallas_call(functools.partial(main_kernel, half=half, radix=radix, kp=...  3 us
  transfers between devices with their start and end apart: 1, of which 1 were waited for; matrix products, arithmetic and copies ran while one was open for 0% of the time, Pallas kernels for 0%

profile of v4, /device:TPU:0, one launch (start us, length us, event | category | flops | bytes accessed | tf_op | source)
XLA Modules:
  0.0 43.3 jit_solution(16017115156849666993)
XLA Ops:
  0.6 6.6 %pack.1 = bf16[8,304,128]{2,1,0:T(8,128)(2,1)} custom-call(bf16[128,1024]{1,0:T(8,128)(2,1)} %x_ref.1, bf16[128,1024]{1,0:T(8,128)(2,1)} %g_ref.1, f32[24,128]{1,0:T(8,128)} %bitcast.2), custom_call_target="tpu_custom_call" | custom-call | tf_op jit(solution)/shard_map/pack/pallas_call | solution.py:410
  7.2 0.0 copy-start
  7.3 0.0 copy-start.1
  7.3 0.0 copy-start.2
  7.3 0.0 copy-start.3
  7.3 0.0 copy-start.4
  7.3 7.4 %all-to-all-start = ((bf16[8,304,128]{2,1,0:T(8,128)(2,1)}), bf16[8,304,128]{2,1,0:T(8,128)(2,1)S(1)}, u32[]{:S(2)}, u32[]{:S(2)}) async-start(bf16[8,304,128]{2,1,0:T(8,128)(2,1)} %pack.1), calls=%async_computation | async-start | bytes 1245184 | tf_op jit(solution)/shard_map/all_to_all | solution.py:423
  14.7 11.9 %all-to-all-done.recv_ref = bf16[8,304,128]{2,1,0:T(8,128)(2,1)S(1)} async-done(((bf16[8,304,128]{2,1,0:T(8,128)(2,1)}), bf16[8,304,128]{2,1,0:T(8,128)(2,1)S(1)}, u32[]{:S(2)}, u32[]{:S(2)}) %all-to-all-start) | async-done | bytes 622624 | tf_op jit(solution)/shard_map/all_to_all | solution.py:423
  26.6 0.0 copy-done
  26.6 0.0 copy-done.1
  26.6 0.0 copy-done.2
  26.6 0.0 copy-done.3
  26.6 0.0 copy-done.4
  26.6 3.0 %main.1 = bf16[8,184,128]{2,1,0:T(8,128)(2,1)S(1)} custom-call(s32[1]{0:T(128)} %bitcast.place_ref, bf16[8,304,128]{2,1,0:T(8,128)(2,1)S(1)} %all-to-all-done.recv_ref, f32[24,1024]{1,0:T(8,128)S(1)} %copy-done.2, f32[3,1024]{1,0:T(4,128)S(1)} %copy-done.4, bf16[512,256]{1,0:T(8,128)(2,1)S(1)} %copy-done, bf16[512,256]{1,0:T(8,128)(2,1)S(1)} %copy-done.1, ...), custom_call_target="tpu_custom_call" | custom-call | tf_op jit(solution)/shard_map/main/pallas_call | solution.py:430
  29.6 12.9 %all_to_all.10.back_ref = bf16[8,184,128]{2,1,0:T(8,128)(2,1)S(1)} all-to-all(bf16[8,184,128]{2,1,0:T(8,128)(2,1)S(1)} %main.1), channel_id=1, replica_groups=mesh['groups'=2,'ctx'=8,'mp'=2] {'ctx'}, dimensions={0} | all-to-all | bytes 753664 | tf_op jit(solution)/shard_map/all_to_all | solution.py:452
  42.5 0.8 %unpack.1 = (bf16[128,1024]{1,0:T(8,128)(2,1)}, f32[24,1024]{1,0:T(8,128)}, f32[3,1024]{1,0:T(4,128)}) custom-call(bf16[8,184,128]{2,1,0:T(8,128)(2,1)S(1)} %all_to_all.10.back_ref), custom_call_target="tpu_custom_call" | custom-call | tf_op jit(solution)/shard_map/unpack/pallas_call | solution.py:454
Async XLA Ops:
  7.2 19.3 %copy-start = (bf16[512,256]{1,0:T(8,128)(2,1)S(1)}, bf16[512,256]{1,0:T(8,128)(2,1)}, u32[]{:S(2)}) copy-start(bf16[512,256]{1,0:T(8,128)(2,1)} %constant.12.clone.wf_ref) | copy-start | bytes 786436
  7.3 19.3 %copy-start.1 = (bf16[512,256]{1,0:T(8,128)(2,1)S(1)}, bf16[512,256]{1,0:T(8,128)(2,1)}, u32[]{:S(2)}) copy-start(bf16[512,256]{1,0:T(8,128)(2,1)} %constant.13.clone.wi_ref) | copy-start | bytes 786436
  7.3 19.3 %copy-start.2 = (f32[24,1024]{1,0:T(8,128)S(1)}, f32[24,1024]{1,0:T(8,128)}, u32[]{:S(2)}) copy-start(f32[24,1024]{1,0:T(8,128)} %mix_ref.1) | copy-start | bytes 294916
  7.3 19.3 %copy-start.3 = (f32[144,128]{1,0:T(8,128)S(1)}, f32[144,128]{1,0:T(8,128)}, u32[]{:S(2)}) copy-start(f32[144,128]{1,0:T(8,128)} %constant.14.clone.tw_ref) | copy-start | bytes 221188
  7.3 19.3 %copy-start.4 = (f32[3,1024]{1,0:T(4,128)S(1)}, f32[3,1024]{1,0:T(4,128)}, u32[]{:S(2)}) copy-start(f32[3,1024]{1,0:T(4,128)} %ar_ref.1) | copy-start | bytes 36868
  7.3 19.3 %all-to-all-start = ((bf16[8,304,128]{2,1,0:T(8,128)(2,1)}), bf16[8,304,128]{2,1,0:T(8,128)(2,1)S(1)}, u32[]{:S(2)}, u32[]{:S(2)}) async-start(bf16[8,304,128]{2,1,0:T(8,128)(2,1)} %pack.1), calls=%async_computation | async-start | bytes 1245184 | tf_op jit(solution)/shard_map/all_to_all | solution.py:423

commit v5 on v4

--- a/solution.py
+++ b/solution.py
@@ -216,17 +216,17 @@
     return first[:both] + first[both:] + dot(w_ref[:both, :], low_ref[:, lanes])
 
 
-def pack_kernel(x_ref, g_ref, f_ref, send_ref, buf, fbuf, in_sem, out_sem, *, wait):
-    count, rows, _ = send_ref.shape
+def pack_kernel(place_ref, x_ref, g_ref, f_ref, send_ref, fbuf, sems, *, wait):
+    count = send_ref.shape[0]
     tok = x_ref.shape[0]
-    taps_in = pltpu.make_async_copy(f_ref, fbuf, in_sem.at[2 * count])
+    taps_in = pltpu.make_async_copy(f_ref, fbuf, sems.at[2 * count])
     taps_in.start()
     copies = []
     for j in range(count):
         lanes = pl.ds(j * LANES, LANES)
         for side, src in enumerate((x_ref, g_ref)):
             copy = pltpu.make_async_copy(
-                src.at[:, lanes], buf.at[j, pl.ds(side * tok, tok), :], in_sem.at[2 * j + side]
+                src.at[:, lanes], send_ref.at[j, pl.ds(side * tok, tok), :], sems.at[2 * j + side]
             )
             copy.start()
             copies.append(copy)
@@ -239,16 +239,9 @@
     high, low = split_pair(fbuf[...])
     pieces = jnp.concatenate([high.astype(f32), low.astype(f32)], axis=0).astype(bf16)
     for j in range(count):
-        buf[j, 2 * tok :, :] = pieces
-    sends = []
-    for j in range(count):
-        copies[2 * j].wait()
-        copies[2 * j + 1].wait()
-        send = pltpu.make_async_copy(buf.at[j], send_ref.at[j], out_sem.at[j])
-        send.start()
-        sends.append(send)
-    for send in sends:
-        send.wait()
+        send_ref[j, 2 * tok :, :] = pieces
+    for copy in copies:
+        copy.wait()
 
 
 def main_kernel(
@@ -378,17 +371,29 @@
         out_ref[j, radix:, :] = pieces
 
 
-def unpack_kernel(back_ref, out_ref, mix_ref, ar_ref):
+def unpack_kernel(back_ref, out_ref, mix_ref, ar_ref, mix_buf, ar_buf, sems):
+    count = back_ref.shape[0]
     tok = out_ref.shape[0]
     taps, order = mix_ref.shape[0], ar_ref.shape[0]
     used = taps + order
-    for j in range(back_ref.shape[0]):
+    copies = []
+    for j in range(count):
+        lanes = pl.ds(j * LANES, LANES)
+        copy = pltpu.make_async_copy(back_ref.at[j, pl.ds(0, tok), :], out_ref.at[:, lanes], sems.at[j])
+        copy.start()
+        copies.append(copy)
+    for j in range(count):
         lanes = slice(j * LANES, (j + 1) * LANES)
-        out_ref[:, lanes] = back_ref[j, 0:tok, :]
         pieces = back_ref[j, tok:, :].astype(f32)
         grads = pieces[0:used] + pieces[used : 2 * used]
-        mix_ref[:, lanes] = grads[0:taps]
-        ar_ref[:, lanes] = grads[taps:used]
+        mix_buf[:, lanes] = grads[0:taps]
+        ar_buf[:, lanes] = grads[taps:used]
+    for buf, ref, place in ((mix_buf, mix_ref, count), (ar_buf, ar_ref, count + 1)):
+        copy = pltpu.make_async_copy(buf, ref, sems.at[place])
+        copy.start()
+        copies.append(copy)
+    for copy in copies:
+        copy.wait()
 
 
 def shape_of(*dims, dtype=f32):
@@ -407,23 +412,23 @@
     swap = functools.partial(lax.all_to_all, axis_name="ctx", split_axis=0, concat_axis=0, tiled=True)
     small = pltpu.CompilerParams(vmem_limit_bytes=8 << 20)
 
+    place = lax.axis_index("ctx").astype(jnp.int32).reshape(1)
+    stay = functools.partial(pltpu.with_memory_space_constraint, memory_space=pltpu.HBM)
     send = pl.pallas_call(
         functools.partial(pack_kernel, wait=STAGGER_NS),
         out_shape=shape_of(count, rows, LANES, dtype=bf16),
-        in_specs=[pl.BlockSpec(memory_space=pl.ANY)] * 3,
-        out_specs=pl.BlockSpec(memory_space=pl.ANY),
+        in_specs=[pl.BlockSpec(memory_space=pltpu.SMEM)] + [pl.BlockSpec(memory_space=pltpu.HBM)] * 3,
+        out_specs=pl.BlockSpec(memory_space=pltpu.VMEM),
         scratch_shapes=[
-            pltpu.VMEM((count, rows, LANES), bf16),
             pltpu.VMEM((taps, tok_rows), f32),
             pltpu.SemaphoreType.DMA((2 * count + 1,)),
-            pltpu.SemaphoreType.DMA((count,)),
         ],
+        compiler_params=small,
         name="pack",
-    )(inputs, cotangent, filters.T)
+    )(place, stay(inputs), stay(cotangent), stay(filters.T))
     recv = swap(send)
 
     whole = lambda *dims: pl.BlockSpec(dims, lambda i, place: (0,) * len(dims))
-    place = lax.axis_index("ctx").astype(jnp.int32).reshape(1)
     span = half * LANES
     split = pltpu.VMEM((2 * radix, span), bf16)
     tall = pltpu.VMEM((half * 2 * radix, LANES), bf16)
@@ -458,6 +463,13 @@
             shape_of(taps, local_width),
             shape_of(order, local_width),
         ),
+        in_specs=[pl.BlockSpec(memory_space=pltpu.VMEM)],
+        out_specs=[pl.BlockSpec(memory_space=pl.ANY)] * 3,
+        scratch_shapes=[
+            pltpu.VMEM((taps, local_width), f32),
+            pltpu.VMEM((order, local_width), f32),
+            pltpu.SemaphoreType.DMA((count + 2,)),
+        ],
         compiler_params=small,
         name="unpack",
     )(back)

time: 43.6 us -> 42.8 us (0.982)
  blocking collectives: 12.9 us -> 32 us
  waiting for transfers between devices: 11.9 us -> 0 us
  starting transfers between devices: 7.42 us -> 0 us
  Pallas kernels: 10.4 us -> 9.71 us
    all_to_all x0 -> x1, blocking collectives: none -> 19.8 us  [local_tiled(): recv = swap(send)]
    all_to_all x1 -> x0, waiting for transfers between devices: 11.9 us -> none  [local_tiled(): recv = swap(send)]
    all_to_all x1 -> x0, starting transfers between devices: 7.42 us -> none  [local_tiled(): recv = swap(send)]
    pallas_call x1, Pallas kernels: 6.61 us -> 5.72 us  [local_tiled(): pl.pallas_call(functools.partial(pack_kernel, wait=STAGGER_NS), out_shape...]
    all_to_all x1, blocking collectives: 12.9 us -> 12.3 us  [local_tiled(): back = swap(result)]
  transfers between devices with their start and end apart: 1 -> 0, of which waited for: 1 -> 0; matrix products, arithmetic and copies ran while one was open for 0% -> 0% of each run, Pallas kernels for 0% -> 0%
where the time goes in v5:
time: 42.8 us; the launch traced here: 42.5 us
  blocking collectives  32 us (75%)
  Pallas kernels  9.71 us (23%)
  between operations  0.71 us (2%)
    all_to_all x1, blocking collectives, local_tiled(): recv = swap(send)  19.8 us
    all_to_all x1, blocking collectives, local_tiled(): back = swap(result)  12.3 us
    pallas_call x1, Pallas kernels, local_tiled(): pl.pallas_call(functools.partial(pack_kernel, wait=STAGGER_NS), out_shape...  5.72 us
    pallas_call x1, Pallas kernels, local_tiled(): pl.pallas_call(functools.partial(main_kernel, half=half, radix=radix, kp=...  3.17 us

profile of v5, /device:TPU:0, one launch (start us, length us, event | category | flops | bytes accessed | tf_op | source)
XLA Modules:
  0.0 42.5 jit_solution(10154958137646534803)
XLA Ops:
  0.6 5.7 %pack.1 = bf16[8,304,128]{2,1,0:T(8,128)(2,1)S(1)} custom-call(s32[1]{0:T(128)} %bitcast.place_ref, bf16[128,1024]{1,0:T(8,128)(2,1)} %x_ref.1, bf16[128,1024]{1,0:T(8,128)(2,1)} %g_ref.1, f32[24,128]{1,0:T(8,128)} %bitcast.2), custom_call_target="tpu_custom_call" | custom-call | tf_op jit(solution)/shard_map/pack/pallas_call | solution.py:417
  6.4 0.0 copy-start
  6.4 0.0 copy-start.1
  6.4 0.0 copy-start.2
  6.4 0.0 copy-start.3
  6.4 0.0 copy-start.4
  6.4 19.8 %all_to_all.10.recv_ref = bf16[8,304,128]{2,1,0:T(8,128)(2,1)S(1)} all-to-all(bf16[8,304,128]{2,1,0:T(8,128)(2,1)S(1)} %pack.1), channel_id=1, replica_groups=mesh['groups'=2,'ctx'=8,'mp'=2] {'ctx'}, dimensions={0} | all-to-all | bytes 1245184 | tf_op jit(solution)/shard_map/all_to_all | solution.py:429
  26.2 0.0 copy-done
  26.2 0.0 copy-done.1
  26.2 0.0 copy-done.2
  26.2 0.0 copy-done.3
  26.2 0.0 copy-done.4
  26.2 3.2 %main.1 = bf16[8,184,128]{2,1,0:T(8,128)(2,1)S(1)} custom-call(s32[1]{0:T(128)} %bitcast.place_ref, bf16[8,304,128]{2,1,0:T(8,128)(2,1)S(1)} %all_to_all.10.recv_ref, f32[24,1024]{1,0:T(8,128)S(1)} %copy-done.2, f32[3,1024]{1,0:T(4,128)S(1)} %copy-done.4, bf16[512,256]{1,0:T(8,128)(2,1)S(1)} %copy-done.1, bf16[512,256]{1,0:T(8,128)(2,1)S(1)} %copy-done, ...), custom_call_target="tpu_custom_call" | custom-call | tf_op jit(solution)/shard_map/main/pallas_call | solution.py:435
  29.4 12.3 %all_to_all.11.back_ref = bf16[8,184,128]{2,1,0:T(8,128)(2,1)S(1)} all-to-all(bf16[8,184,128]{2,1,0:T(8,128)(2,1)S(1)} %main.1), channel_id=1, replica_groups=mesh['groups'=2,'ctx'=8,'mp'=2] {'ctx'}, dimensions={0} | all-to-all | bytes 753664 | tf_op jit(solution)/shard_map/all_to_all | solution.py:457
  41.7 0.8 %unpack.1 = (bf16[128,1024]{1,0:T(8,128)(2,1)}, f32[24,1024]{1,0:T(8,128)}, f32[3,1024]{1,0:T(4,128)}) custom-call(bf16[8,184,128]{2,1,0:T(8,128)(2,1)S(1)} %all_to_all.11.back_ref), custom_call_target="tpu_custom_call" | custom-call | tf_op jit(solution)/shard_map/unpack/pallas_call | solution.py:459
Async XLA Ops:
  6.4 19.8 %copy-start = (bf16[512,256]{1,0:T(8,128)(2,1)S(1)}, bf16[512,256]{1,0:T(8,128)(2,1)}, u32[]{:S(2)}) copy-start(bf16[512,256]{1,0:T(8,128)(2,1)} %constant.13.clone.wi_ref) | copy-start | bytes 786436
  6.4 19.8 %copy-start.1 = (bf16[512,256]{1,0:T(8,128)(2,1)S(1)}, bf16[512,256]{1,0:T(8,128)(2,1)}, u32[]{:S(2)}) copy-start(bf16[512,256]{1,0:T(8,128)(2,1)} %constant.12.clone.wf_ref) | copy-start | bytes 786436
  6.4 19.8 %copy-start.2 = (f32[24,1024]{1,0:T(8,128)S(1)}, f32[24,1024]{1,0:T(8,128)}, u32[]{:S(2)}) copy-start(f32[24,1024]{1,0:T(8,128)} %mix_ref.1) | copy-start | bytes 294916
  6.4 19.8 %copy-start.3 = (f32[144,128]{1,0:T(8,128)S(1)}, f32[144,128]{1,0:T(8,128)}, u32[]{:S(2)}) copy-start(f32[144,128]{1,0:T(8,128)} %constant.14.clone.tw_ref) | copy-start | bytes 221188
  6.4 19.8 %copy-start.4 = (f32[3,1024]{1,0:T(4,128)S(1)}, f32[3,1024]{1,0:T(4,128)}, u32[]{:S(2)}) copy-start(f32[3,1024]{1,0:T(4,128)} %ar_ref.1) | copy-start | bytes 36868

commit v6 on v5

--- a/solution.py
+++ b/solution.py
@@ -198,9 +198,9 @@
     return jnp.dot(a, b, preferred_element_type=f32)
 
 
-def outer_forward(src_ref, start, tw_ref, high_ref, low_ref, half, radix):
+def outer_forward(src_ref, start, tw_ref, high_ref, low_ref, half, radix, slot):
     for r in range(0, radix, ROWS):
-        parts = half_forward([src_ref[h, start + r : start + r + ROWS, :].astype(f32) for h in range(half)])
+        parts = half_forward([src_ref[slot[h], start + r : start + r + ROWS, :].astype(f32) for h in range(half)])
         for k, (re, im) in enumerate(parts):
             c, s = tw_ref[r : r + ROWS, k : k + 1], tw_ref[r : r + ROWS, half + k : half + k + 1]
             lanes = slice(k * LANES, (k + 1) * LANES)
@@ -216,7 +216,7 @@
     return first[:both] + first[both:] + dot(w_ref[:both, :], low_ref[:, lanes])
 
 
-def pack_kernel(place_ref, x_ref, g_ref, f_ref, send_ref, fbuf, sems, *, wait):
+def pack_kernel(place_ref, x_ref, g_ref, f_ref, send_ref, fbuf, sems, *, wait, slot):
     count = send_ref.shape[0]
     tok = x_ref.shape[0]
     taps_in = pltpu.make_async_copy(f_ref, fbuf, sems.at[2 * count])
@@ -226,7 +226,7 @@
         lanes = pl.ds(j * LANES, LANES)
         for side, src in enumerate((x_ref, g_ref)):
             copy = pltpu.make_async_copy(
-                src.at[:, lanes], send_ref.at[j, pl.ds(side * tok, tok), :], sems.at[2 * j + side]
+                src.at[:, lanes], send_ref.at[slot[j], pl.ds(side * tok, tok), :], sems.at[2 * j + side]
             )
             copy.start()
             copies.append(copy)
@@ -265,6 +265,7 @@
     half,
     radix,
     kp,
+    slot,
 ):
     taps = mix_ref.shape[0]
     order = ar_ref.shape[0]
@@ -272,7 +273,7 @@
     scale = 1.0 / (half * radix)
     blocks = []
     for h in range(half):
-        both = recv_ref[h, 2 * radix : 2 * radix + 2 * taps, :].astype(f32)
+        both = recv_ref[slot[h], 2 * radix : 2 * radix + 2 * taps, :].astype(f32)
         value = both[:taps] + both[taps:]
         extra = jnp.zeros((kp - taps, radix), f32)
         if h == 0:
@@ -313,7 +314,7 @@
     d_high, d_low = diagonal(m_high), diagonal(m_low)
     mixer = jnp.concatenate([d_high, d_high, d_low], axis=0)
 
-    outer_forward(recv_ref, 0, tw_ref, b_high, b_low, half, radix)
+    outer_forward(recv_ref, 0, tw_ref, b_high, b_low, half, radix, slot)
     for m in range(half // 2):
         lanes = slice(m * 2 * LANES, (m + 1) * 2 * LANES)
         rows = slice(2 * m * kp, 2 * (m + 1) * kp)
@@ -343,9 +344,9 @@
             c, s = tw_ref[r : r + ROWS, k : k + 1], tw_ref[r : r + ROWS, half + k : half + k + 1]
             us.append((gr * c - gi * s, gr * s + gi * c))
         for h, value in enumerate(half_inverse(us)):
-            out_ref[h, r : r + ROWS, :] = value.astype(bf16)
-
-    outer_forward(recv_ref, radix, tw_ref, b_high, b_low, half, radix)
+            out_ref[slot[h], r : r + ROWS, :] = value.astype(bf16)
+
+    outer_forward(recv_ref, radix, tw_ref, b_high, b_low, half, radix, slot)
     for m in range(half // 2):
         lanes = slice(m * 2 * LANES, (m + 1) * 2 * LANES)
         cot = inner_dft(wf_ref, b_high, b_low, lanes)
@@ -371,7 +372,7 @@
         out_ref[j, radix:, :] = pieces
 
 
-def unpack_kernel(back_ref, out_ref, mix_ref, ar_ref, mix_buf, ar_buf, sems):
+def unpack_kernel(back_ref, out_ref, mix_ref, ar_ref, mix_buf, ar_buf, sems, *, slot):
     count = back_ref.shape[0]
     tok = out_ref.shape[0]
     taps, order = mix_ref.shape[0], ar_ref.shape[0]
@@ -379,12 +380,12 @@
     copies = []
     for j in range(count):
         lanes = pl.ds(j * LANES, LANES)
-        copy = pltpu.make_async_copy(back_ref.at[j, pl.ds(0, tok), :], out_ref.at[:, lanes], sems.at[j])
+        copy = pltpu.make_async_copy(back_ref.at[slot[j], pl.ds(0, tok), :], out_ref.at[:, lanes], sems.at[j])
         copy.start()
         copies.append(copy)
     for j in range(count):
         lanes = slice(j * LANES, (j + 1) * LANES)
-        pieces = back_ref[j, tok:, :].astype(f32)
+        pieces = back_ref[slot[j], tok:, :].astype(f32)
         grads = pieces[0:used] + pieces[used : 2 * used]
         mix_buf[:, lanes] = grads[0:taps]
         ar_buf[:, lanes] = grads[taps:used]
@@ -409,13 +410,22 @@
     wf, wi, twist = dft_constants(half, radix)
     rows = 2 * tok_rows + 2 * taps
     back_rows = -(-(tok_rows + 2 * (taps + order)) // 8) * 8
-    swap = functools.partial(lax.all_to_all, axis_name="ctx", split_axis=0, concat_axis=0, tiled=True)
+    ranks = list(range(count))[::-1]
+    slot = [ranks.index(i) for i in range(count)]
+    swap = functools.partial(
+        lax.all_to_all,
+        axis_name="ctx",
+        split_axis=0,
+        concat_axis=0,
+        tiled=True,
+        axis_index_groups=[ranks],
+    )
     small = pltpu.CompilerParams(vmem_limit_bytes=8 << 20)
 
     place = lax.axis_index("ctx").astype(jnp.int32).reshape(1)
     stay = functools.partial(pltpu.with_memory_space_constraint, memory_space=pltpu.HBM)
     send = pl.pallas_call(
-        functools.partial(pack_kernel, wait=STAGGER_NS),
+        functools.partial(pack_kernel, wait=STAGGER_NS, slot=slot),
         out_shape=shape_of(count, rows, LANES, dtype=bf16),
         in_specs=[pl.BlockSpec(memory_space=pltpu.SMEM)] + [pl.BlockSpec(memory_space=pltpu.HBM)] * 3,
         out_specs=pl.BlockSpec(memory_space=pltpu.VMEM),
@@ -433,7 +443,7 @@
     split = pltpu.VMEM((2 * radix, span), bf16)
     tall = pltpu.VMEM((half * 2 * radix, LANES), bf16)
     result = pl.pallas_call(
-        functools.partial(main_kernel, half=half, radix=radix, kp=kp),
+        functools.partial(main_kernel, half=half, radix=radix, kp=kp, slot=slot),
         out_shape=shape_of(count, back_rows, LANES, dtype=bf16),
         grid_spec=pltpu.PrefetchScalarGridSpec(
             num_scalar_prefetch=1,
@@ -457,7 +467,7 @@
     back = swap(result)
 
     return pl.pallas_call(
-        unpack_kernel,
+        functools.partial(unpack_kernel, slot=slot),
         out_shape=(
             shape_of(tok_rows, local_width, dtype=bf16),
             shape_of(taps, local_width),

time: 42.8 us -> 41.7 us (0.974)
  blocking collectives: 32 us -> 31 us
    all_to_all x1, blocking collectives: 19.8 us -> 18.5 us  [local_tiled(): recv = swap(send)]
where the time goes in v6:
time: 41.7 us; the launch traced here: 41.4 us
  blocking collectives  31 us (74%)
  Pallas kernels  9.72 us (23%)
  between operations  0.71 us (2%)
    all_to_all x1, blocking collectives, local_tiled(): recv = swap(send)  18.5 us
    all_to_all x1, blocking collectives, local_tiled(): back = swap(result)  12.5 us
    pallas_call x1, Pallas kernels, local_tiled(): pl.pallas_call(functools.partial(pack_kernel, wait=STAGGER_NS, slot=slot)...  5.72 us
    pallas_call x1, Pallas kernels, local_tiled(): pl.pallas_call(functools.partial(main_kernel, half=half, radix=radix, kp=...  3.19 us

profile of v6, /device:TPU:0, one launch (start us, length us, event | category | flops | bytes accessed | tf_op | source)
XLA Modules:
  0.0 41.4 jit_solution(9256919862521971954)
XLA Ops:
  0.6 5.7 %pack.1 = bf16[8,304,128]{2,1,0:T(8,128)(2,1)S(1)} custom-call(s32[1]{0:T(128)} %bitcast.place_ref, bf16[128,1024]{1,0:T(8,128)(2,1)} %x_ref.1, bf16[128,1024]{1,0:T(8,128)(2,1)} %g_ref.1, f32[24,128]{1,0:T(8,128)} %bitcast.2), custom_call_target="tpu_custom_call" | custom-call | tf_op jit(solution)/shard_map/pack/pallas_call | solution.py:427
  6.4 0.0 copy-start
  6.4 0.0 copy-start.1
  6.4 0.0 copy-start.2
  6.4 0.0 copy-start.3
  6.4 0.0 copy-start.4
  6.4 18.5 %all_to_all.10.recv_ref = bf16[8,304,128]{2,1,0:T(8,128)(2,1)S(1)} all-to-all(bf16[8,304,128]{2,1,0:T(8,128)(2,1)S(1)} %pack.1), channel_id=1, replica_groups={{14,12,10,8,6,4,2,0},{15,13,11,9,7,5,3,1},{30,28,26,24,22,20,18,16},{31..., dimensions={0} | all-to-all | bytes 1245184 | tf_op jit(solution)/shard_map/all_to_all | solution.py:439
  24.9 0.0 copy-done
  24.9 0.0 copy-done.1
  24.9 0.0 copy-done.2
  24.9 0.0 copy-done.3
  24.9 0.0 copy-done.4
  24.9 3.2 %main.1 = bf16[8,184,128]{2,1,0:T(8,128)(2,1)S(1)} custom-call(s32[1]{0:T(128)} %bitcast.place_ref, bf16[8,304,128]{2,1,0:T(8,128)(2,1)S(1)} %all_to_all.10.recv_ref, f32[24,1024]{1,0:T(8,128)S(1)} %copy-done.2, f32[3,1024]{1,0:T(4,128)S(1)} %copy-done.4, bf16[512,256]{1,0:T(8,128)(2,1)S(1)} %copy-done.1, bf16[512,256]{1,0:T(8,128)(2,1)S(1)} %copy-done, ...), custom_call_target="tpu_custom_call" | custom-call | tf_op jit(solution)/shard_map/main/pallas_call | solution.py:445
  28.1 12.5 %all_to_all.11.back_ref = bf16[8,184,128]{2,1,0:T(8,128)(2,1)S(1)} all-to-all(bf16[8,184,128]{2,1,0:T(8,128)(2,1)S(1)} %main.1), channel_id=1, replica_groups={{14,12,10,8,6,4,2,0},{15,13,11,9,7,5,3,1},{30,28,26,24,22,20,18,16},{31..., dimensions={0} | all-to-all | bytes 753664 | tf_op jit(solution)/shard_map/all_to_all | solution.py:467
  40.6 0.8 %unpack.1 = (bf16[128,1024]{1,0:T(8,128)(2,1)}, f32[24,1024]{1,0:T(8,128)}, f32[3,1024]{1,0:T(4,128)}) custom-call(bf16[8,184,128]{2,1,0:T(8,128)(2,1)S(1)} %all_to_all.11.back_ref), custom_call_target="tpu_custom_call" | custom-call | tf_op jit(solution)/shard_map/unpack/pallas_call | solution.py:469
Async XLA Ops:
  6.4 18.5 %copy-start = (bf16[512,256]{1,0:T(8,128)(2,1)S(1)}, bf16[512,256]{1,0:T(8,128)(2,1)}, u32[]{:S(2)}) copy-start(bf16[512,256]{1,0:T(8,128)(2,1)} %constant.13.clone.wi_ref) | copy-start | bytes 786436
  6.4 18.5 %copy-start.1 = (bf16[512,256]{1,0:T(8,128)(2,1)S(1)}, bf16[512,256]{1,0:T(8,128)(2,1)}, u32[]{:S(2)}) copy-start(bf16[512,256]{1,0:T(8,128)(2,1)} %constant.12.clone.wf_ref) | copy-start | bytes 786436
  6.4 18.5 %copy-start.2 = (f32[24,1024]{1,0:T(8,128)S(1)}, f32[24,1024]{1,0:T(8,128)}, u32[]{:S(2)}) copy-start(f32[24,1024]{1,0:T(8,128)} %mix_ref.1) | copy-start | bytes 294916
  6.4 18.5 %copy-start.3 = (f32[144,128]{1,0:T(8,128)S(1)}, f32[144,128]{1,0:T(8,128)}, u32[]{:S(2)}) copy-start(f32[144,128]{1,0:T(8,128)} %constant.14.clone.tw_ref) | copy-start | bytes 221188
  6.4 18.5 %copy-start.4 = (f32[3,1024]{1,0:T(4,128)S(1)}, f32[3,1024]{1,0:T(4,128)}, u32[]{:S(2)}) copy-start(f32[3,1024]{1,0:T(4,128)} %ar_ref.1) | copy-start | bytes 36868

commit v7 on v6

--- a/solution.py
+++ b/solution.py
@@ -410,7 +410,7 @@
     wf, wi, twist = dft_constants(half, radix)
     rows = 2 * tok_rows + 2 * taps
     back_rows = -(-(tok_rows + 2 * (taps + order)) // 8) * 8
-    ranks = list(range(count))[::-1]
+    ranks = [i ^ (i >> 1) for i in range(count)][::-1]
     slot = [ranks.index(i) for i in range(count)]
     swap = functools.partial(
         lax.all_to_all,

time: 41.7 us -> 40 us (0.959)
  blocking collectives: 31 us -> 29.2 us
    all_to_all x1, blocking collectives: 12.5 us -> 11.1 us  [local_tiled(): back = swap(result)]
where the time goes in v7:
time: 40 us; the launch traced here: 39.7 us
  blocking collectives  29.2 us (73%)
  Pallas kernels  9.73 us (24%)
  between operations  0.71 us (2%)
    all_to_all x1, blocking collectives, local_tiled(): recv = swap(send)  18.1 us
    all_to_all x1, blocking collectives, local_tiled(): back = swap(result)  11.1 us
    pallas_call x1, Pallas kernels, local_tiled(): pl.pallas_call(functools.partial(pack_kernel, wait=STAGGER_NS, slot=slot)...  5.72 us
    pallas_call x1, Pallas kernels, local_tiled(): pl.pallas_call(functools.partial(main_kernel, half=half, radix=radix, kp=...  3.2 us
    pallas_call x1, Pallas kernels, local_tiled(): pl.pallas_call(functools.partial(unpack_kernel, slot=slot), out_shape=(sh...  0.82 us

profile of v7, /device:TPU:0, one launch (start us, length us, event | category | flops | bytes accessed | tf_op | source)
XLA Modules:
  0.0 39.7 jit_solution(9118637744899243479)
XLA Ops:
  0.6 5.7 %pack.1 = bf16[8,304,128]{2,1,0:T(8,128)(2,1)S(1)} custom-call(s32[1]{0:T(128)} %bitcast.place_ref, bf16[128,1024]{1,0:T(8,128)(2,1)} %x_ref.1, bf16[128,1024]{1,0:T(8,128)(2,1)} %g_ref.1, f32[24,128]{1,0:T(8,128)} %bitcast.2), custom_call_target="tpu_custom_call" | custom-call | tf_op jit(solution)/shard_map/pack/pallas_call | solution.py:427
  6.4 0.0 copy-start
  6.4 0.0 copy-start.1
  6.4 0.0 copy-start.2
  6.4 0.0 copy-start.3
  6.4 0.0 copy-start.4
  6.4 18.1 %all_to_all.10.recv_ref = bf16[8,304,128]{2,1,0:T(8,128)(2,1)S(1)} all-to-all(bf16[8,304,128]{2,1,0:T(8,128)(2,1)S(1)} %pack.1), channel_id=1, replica_groups={{8,10,14,12,4,6,2,0},{9,11,15,13,5,7,3,1},{24,26,30,28,20,22,18,16},{25..., dimensions={0} | all-to-all | bytes 1245184 | tf_op jit(solution)/shard_map/all_to_all | solution.py:439
  24.5 0.0 copy-done
  24.5 0.0 copy-done.1
  24.5 0.0 copy-done.2
  24.5 0.0 copy-done.3
  24.5 0.0 copy-done.4
  24.5 3.2 %main.1 = bf16[8,184,128]{2,1,0:T(8,128)(2,1)S(1)} custom-call(s32[1]{0:T(128)} %bitcast.place_ref, bf16[8,304,128]{2,1,0:T(8,128)(2,1)S(1)} %all_to_all.10.recv_ref, f32[24,1024]{1,0:T(8,128)S(1)} %copy-done.2, f32[3,1024]{1,0:T(4,128)S(1)} %copy-done.4, bf16[512,256]{1,0:T(8,128)(2,1)S(1)} %copy-done.1, bf16[512,256]{1,0:T(8,128)(2,1)S(1)} %copy-done, ...), custom_call_target="tpu_custom_call" | custom-call | tf_op jit(solution)/shard_map/main/pallas_call | solution.py:445
  27.8 11.1 %all_to_all.11.back_ref = bf16[8,184,128]{2,1,0:T(8,128)(2,1)S(1)} all-to-all(bf16[8,184,128]{2,1,0:T(8,128)(2,1)S(1)} %main.1), channel_id=1, replica_groups={{8,10,14,12,4,6,2,0},{9,11,15,13,5,7,3,1},{24,26,30,28,20,22,18,16},{25..., dimensions={0} | all-to-all | bytes 753664 | tf_op jit(solution)/shard_map/all_to_all | solution.py:467
  38.9 0.8 %unpack.1 = (bf16[128,1024]{1,0:T(8,128)(2,1)}, f32[24,1024]{1,0:T(8,128)}, f32[3,1024]{1,0:T(4,128)}) custom-call(bf16[8,184,128]{2,1,0:T(8,128)(2,1)S(1)} %all_to_all.11.back_ref), custom_call_target="tpu_custom_call" | custom-call | tf_op jit(solution)/shard_map/unpack/pallas_call | solution.py:469
Async XLA Ops:
  6.4 18.2 %copy-start = (bf16[512,256]{1,0:T(8,128)(2,1)S(1)}, bf16[512,256]{1,0:T(8,128)(2,1)}, u32[]{:S(2)}) copy-start(bf16[512,256]{1,0:T(8,128)(2,1)} %constant.13.clone.wi_ref) | copy-start | bytes 786436
  6.4 18.1 %copy-start.1 = (bf16[512,256]{1,0:T(8,128)(2,1)S(1)}, bf16[512,256]{1,0:T(8,128)(2,1)}, u32[]{:S(2)}) copy-start(bf16[512,256]{1,0:T(8,128)(2,1)} %constant.12.clone.wf_ref) | copy-start | bytes 786436
  6.4 18.1 %copy-start.2 = (f32[24,1024]{1,0:T(8,128)S(1)}, f32[24,1024]{1,0:T(8,128)}, u32[]{:S(2)}) copy-start(f32[24,1024]{1,0:T(8,128)} %mix_ref.1) | copy-start | bytes 294916
  6.4 18.1 %copy-start.3 = (f32[144,128]{1,0:T(8,128)S(1)}, f32[144,128]{1,0:T(8,128)}, u32[]{:S(2)}) copy-start(f32[144,128]{1,0:T(8,128)} %constant.14.clone.tw_ref) | copy-start | bytes 221188
  6.4 18.1 %copy-start.4 = (f32[3,1024]{1,0:T(4,128)S(1)}, f32[3,1024]{1,0:T(4,128)}, u32[]{:S(2)}) copy-start(f32[3,1024]{1,0:T(4,128)} %ar_ref.1) | copy-start | bytes 36868
